TPU v7x, 32 devices: a whole 2x2x4 slice. The times are simulated.
32 devices in a mesh: seq: 8 (over y, x, core), fsdp: 4 (over z).
Axes of the slice: x: 2, y: 2, z: 4, core: 2. Of those that a mesh axis runs over, the one named last changes fastest.
Arguments:
- tokens: bfloat16 [12, 1376, 1024], P('fsdp', 'seq'), may hold values from -16 to 16
- cotangent: bfloat16 [12, 1376, 1024], P('fsdp', 'seq'), may hold values from -6 to 6
- lengths: int32 [12], P('fsdp'), may hold values from 688 to 1370, as said below
- joint_weight: bfloat16 [1024, 3072], P(('seq', 'fsdp')), may hold values from -6 to 6
- output_weight: bfloat16 [1024, 1024], P(('seq', 'fsdp')), may hold values from -1.5 to 1.5
- expand_weight: bfloat16 [1024, 4096], P(('seq', 'fsdp')), may hold values from -0.1875 to 0.1875
- reduce_weight: bfloat16 [4096, 1024], P(('seq', 'fsdp')), may hold values from -0.09375 to 0.09375
- vectors: bfloat16 [10, 1024], P(None, ('seq', 'fsdp')), may hold values from -1.7 to 1.8
- expand_bias: bfloat16 [4096], P(('seq', 'fsdp')), may hold values from -0.59765625 to 0.59765625
- first_joint: float32 [1024, 3072], P(('seq', 'fsdp')), may hold values from -46.25965 to 46.25965
- first_output: float32 [1024, 1024], P(('seq', 'fsdp')), may hold values from -7.709942 to 7.709942
- first_expand: float32 [1024, 4096], P(('seq', 'fsdp')), may hold values from -23.129826 to 23.129826
- first_reduce: float32 [4096, 1024], P(('seq', 'fsdp')), may hold values from -46.25965 to 46.25965
- first_vectors: float32 [10, 1024], P(None, ('seq', 'fsdp')), may hold values from -77.09942 to 77.09942
- first_bias: float32 [4096], P(('seq', 'fsdp')), may hold values from -23.129826 to 23.129826
- second_joint: float32 [1024, 3072], P(('seq', 'fsdp')), may hold values from 1.6512 to 16.512
- second_output: float32 [1024, 1024], P(('seq', 'fsdp')), may hold values from 0.049536 to 0.49536
- second_expand: float32 [1024, 4096], P(('seq', 'fsdp')), may hold values from 0.49536 to 4.9536
- second_reduce: float32 [4096, 1024], P(('seq', 'fsdp')), may hold values from 1.6512 to 16.512
- second_vectors: float32 [10, 1024], P(None, ('seq', 'fsdp')), may hold values from 4.9536 to 49.536
- second_bias: float32 [4096], P(('seq', 'fsdp')), may hold values from 0.49536 to 4.9536
Outputs:
- block_output: bfloat16 [12, 1376, 1024], P('fsdp', 'seq')
- input_grad: bfloat16 [12, 1376, 1024], P('fsdp', 'seq')
- joint_grad: float32 [1024, 3072], P(('seq', 'fsdp'))
- output_grad: float32 [1024, 1024], P(('seq', 'fsdp'))
- expand_grad: float32 [1024, 4096], P(('seq', 'fsdp'))
- reduce_grad: float32 [4096, 1024], P(('seq', 'fsdp'))
- vector_grad: float32 [10, 1024], P(None, ('seq', 'fsdp'))
- bias_grad: float32 [4096], P(('seq', 'fsdp'))
- joint_new: float32 [1024, 3072], P(('seq', 'fsdp'))
- output_new: float32 [1024, 1024], P(('seq', 'fsdp'))
- expand_new: float32 [1024, 4096], P(('seq', 'fsdp'))
- reduce_new: float32 [4096, 1024], P(('seq', 'fsdp'))
- vector_new: float32 [10, 1024], P(None, ('seq', 'fsdp'))
- bias_new: float32 [4096], P(('seq', 'fsdp'))
- mean_joint: float32 [1024, 3072], P(('seq', 'fsdp'))
- mean_output: float32 [1024, 1024], P(('seq', 'fsdp'))
- mean_expand: float32 [1024, 4096], P(('seq', 'fsdp'))
- mean_reduce: float32 [4096, 1024], P(('seq', 'fsdp'))
- mean_vectors: float32 [10, 1024], P(None, ('seq', 'fsdp'))
- mean_bias: float32 [4096], P(('seq', 'fsdp'))
- square_joint: float32 [1024, 3072], P(('seq', 'fsdp'))
- square_output: float32 [1024, 1024], P(('seq', 'fsdp'))
- square_expand: float32 [1024, 4096], P(('seq', 'fsdp'))
- square_reduce: float32 [4096, 1024], P(('seq', 'fsdp'))
- square_vectors: float32 [10, 1024], P(None, ('seq', 'fsdp'))
- square_bias: float32 [4096], P(('seq', 'fsdp'))
Inputs may be any that keep to these rules, and one draw needn't show every extreme that they name: `lengths`: image 0 has exactly 1370 valid tokens.
All inputs are finite; a program needn't handle non-finite values.
Results may differ from a plain program's by a relative error of at most 0.009.
The roundings to bfloat16 on the way count: a program that leaves them out, or rounds other values in their place, can miss the bound.
Values may be sent and summed in bfloat16 or wider, within the bound.
No kernel may reach another device: no remote copies, remote signals or barrier semaphores. Data moves between devices by JAX's collectives and lax.ppermute only.
A program may use at most 192 MiB of HBM per device.

v0:
```python
import jax
import jax.numpy as jnp
from jax import lax
from jax.sharding import PartitionSpec as P

H = 16
HD = 64
ADAM_STEP = 2


EPS_NORM = 1e-06
MASK_LOW = -1e30
BETA_ONE = 0.9
BETA_TWO = 0.999
EPS_ADAM = 1e-08
STEP_RATES = (0.006, 0.05, 0.006, 0.004, 0.15, 0.02)
DECAY_RATES = (0.04, 0.04, 0.04, 0.04, 0.0, 0.0)


def norm_apply(features, gain_row, shift_row):
    average = jnp.mean(features, axis=-1, keepdims=True)
    centered = features - average
    spread = jnp.mean(centered * centered, axis=-1, keepdims=True)
    return centered * lax.rsqrt(spread + EPS_NORM) * gain_row + shift_row


def gelu_exact(values):
    return jax.nn.gelu(values, approximate=False)


def contract_rows(left, right):
    return lax.dot_general(
        left, right, (((0,), (0,)), ((), ())), preferred_element_type=jnp.float32
    )


def times_transpose(left, right):
    return lax.dot_general(
        left, right, (((1,), (1,)), ((), ())), preferred_element_type=jnp.float32
    )


def head_scores(queries, key_rows, valid_len):
    raw_scores = (
        jnp.einsum("qhd,khd->hqk", queries, key_rows, preferred_element_type=jnp.float32) * 0.125
    )
    usable = jnp.arange(key_rows.shape[0]) < valid_len
    return jnp.where(usable[None, None, :], raw_scores, MASK_LOW)


def attend_forward(pieces):
    grouped, valid_len = pieces
    scores = head_scores(grouped[:, 0], grouped[:, 1], valid_len)
    highest = jnp.max(scores, axis=-1, keepdims=True)
    exponent = jnp.exp(scores - highest)
    summed = jnp.sum(exponent, axis=-1, keepdims=True)
    softmax = (exponent / summed).astype(jnp.bfloat16)
    attended = jnp.einsum(
        "hqk,khd->qhd", softmax, grouped[:, 2], preferred_element_type=jnp.float32
    )
    return (attended.astype(jnp.bfloat16), highest + jnp.log(summed))


def attend_backward(pieces):
    grouped, grad_heads, log_total, valid_len = pieces
    queries = grouped[:, 0]
    key_rows = grouped[:, 1]
    value_rows = grouped[:, 2]
    scores = head_scores(queries, key_rows, valid_len)
    softmax = jnp.exp(scores - log_total)
    grad_probs = jnp.einsum(
        "qhd,khd->hqk", grad_heads, value_rows, preferred_element_type=jnp.float32
    )
    grad_values = jnp.einsum(
        "hqk,qhd->khd", softmax.astype(jnp.bfloat16), grad_heads, preferred_element_type=jnp.float32
    )
    inner = jnp.sum(softmax * grad_probs, axis=-1, keepdims=True)
    grad_scores = (softmax * (grad_probs - inner)).astype(jnp.bfloat16)
    grad_queries = (
        jnp.einsum("hqk,khd->qhd", grad_scores, key_rows, preferred_element_type=jnp.float32)
        * 0.125
    )
    grad_keys = (
        jnp.einsum("hqk,qhd->khd", grad_scores, queries, preferred_element_type=jnp.float32) * 0.125
    )
    return jnp.stack([grad_queries, grad_keys, grad_values], axis=1).astype(jnp.bfloat16)


def adam_update(weight, gradient, moment_one, moment_two, step_rate, decay_rate):
    mean_new = BETA_ONE * moment_one + (1.0 - BETA_ONE) * gradient
    square_new = BETA_TWO * moment_two + (1.0 - BETA_TWO) * gradient * gradient
    mean_hat = mean_new / (1.0 - BETA_ONE**ADAM_STEP)
    square_hat = square_new / (1.0 - BETA_TWO**ADAM_STEP)
    weight_f = weight.astype(jnp.float32)
    updated = weight_f - step_rate * (
        mean_hat / (jnp.sqrt(square_hat) + EPS_ADAM) + decay_rate * weight_f
    )
    return (updated, mean_new, square_new)


def body(
    tokens,
    cotangent,
    lengths,
    joint_weight,
    output_weight,
    expand_weight,
    reduce_weight,
    vectors,
    expand_bias,
    first_joint,
    first_output,
    first_expand,
    first_reduce,
    first_vectors,
    first_bias,
    second_joint,
    second_output,
    second_expand,
    second_reduce,
    second_vectors,
    second_bias,
):
    image_count, local_len, model_width = tokens.shape
    gathered = (
        lax.all_gather(joint_weight, ("seq", "fsdp"), axis=0, tiled=True),
        lax.all_gather(output_weight, ("seq", "fsdp"), axis=0, tiled=True),
        lax.all_gather(expand_weight, ("seq", "fsdp"), axis=0, tiled=True),
        lax.all_gather(reduce_weight, ("seq", "fsdp"), axis=0, tiled=True),
        lax.all_gather(vectors, ("seq", "fsdp"), axis=1, tiled=True),
        lax.all_gather(expand_bias, ("seq", "fsdp"), axis=0, tiled=True),
    )
    full_joint, full_output, full_expand, full_reduce, full_vectors, full_bias = gathered
    vector_rows = full_vectors.astype(jnp.float32)
    hidden_bias = full_bias.astype(jnp.float32)
    features = tokens.reshape(-1, model_width).astype(jnp.float32)
    normed, norm_one_back = jax.vjp(norm_apply, features, vector_rows[0], vector_rows[1])
    normed_low = normed.astype(jnp.bfloat16)
    joint_bias = jnp.concatenate([vector_rows[2], jnp.zeros_like(vector_rows[2]), vector_rows[3]])
    joint = jnp.dot(normed_low, full_joint, preferred_element_type=jnp.float32) + joint_bias
    joint_low = joint.astype(jnp.bfloat16).reshape(image_count, local_len, 3, H, HD)
    by_head = lax.all_to_all(joint_low, "seq", split_axis=3, concat_axis=1, tiled=True)
    attended_heads, log_total = lax.map(attend_forward, (by_head, lengths))
    attended_tok = lax.all_to_all(attended_heads, "seq", split_axis=1, concat_axis=2, tiled=True)
    attended_rows = attended_tok.reshape(-1, model_width)
    projected = (
        jnp.dot(attended_rows, full_output, preferred_element_type=jnp.float32) + vector_rows[4]
    )
    hidden_one = features + vector_rows[5] * projected
    normed_two, norm_two_back = jax.vjp(norm_apply, hidden_one, vector_rows[6], vector_rows[7])
    normed_two_low = normed_two.astype(jnp.bfloat16)
    expanded = (
        jnp.dot(normed_two_low, full_expand, preferred_element_type=jnp.float32) + hidden_bias
    )
    activated, gelu_back = jax.vjp(gelu_exact, expanded)
    activated_low = activated.astype(jnp.bfloat16)
    reduced = (
        jnp.dot(activated_low, full_reduce, preferred_element_type=jnp.float32) + vector_rows[8]
    )
    result = hidden_one + vector_rows[9] * reduced
    block_output = result.astype(jnp.bfloat16).reshape(tokens.shape)
    regathered = (
        lax.all_gather(joint_weight, ("seq", "fsdp"), axis=0, tiled=True),
        lax.all_gather(output_weight, ("seq", "fsdp"), axis=0, tiled=True),
        lax.all_gather(expand_weight, ("seq", "fsdp"), axis=0, tiled=True),
        lax.all_gather(reduce_weight, ("seq", "fsdp"), axis=0, tiled=True),
        lax.all_gather(vectors, ("seq", "fsdp"), axis=1, tiled=True),
        lax.all_gather(expand_bias, ("seq", "fsdp"), axis=0, tiled=True),
    )
    full_joint, full_output, full_expand, full_reduce, full_vectors, full_bias = regathered
    vector_rows = full_vectors.astype(jnp.float32)
    positions = lax.axis_index("seq") * local_len + jnp.arange(local_len)
    live_rows = (positions[None, :] < lengths[:, None]).astype(jnp.float32).reshape(-1, 1)
    grad_rows = cotangent.reshape(-1, model_width).astype(jnp.float32) * live_rows
    grad_scale_two = jnp.sum(grad_rows * reduced, axis=0)
    grad_reduced = (grad_rows * vector_rows[9]).astype(jnp.bfloat16)
    grad_reduce_bias = jnp.sum(grad_reduced.astype(jnp.float32), axis=0)
    grad_reduce = contract_rows(activated_low, grad_reduced)
    grad_activated = times_transpose(grad_reduced, full_reduce)
    (grad_expanded,) = gelu_back(grad_activated)
    grad_expanded_low = grad_expanded.astype(jnp.bfloat16)
    grad_hidden_bias = jnp.sum(grad_expanded_low.astype(jnp.float32), axis=0)
    grad_expand = contract_rows(normed_two_low, grad_expanded_low)
    grad_normed_two = times_transpose(grad_expanded_low, full_expand)
    grad_hidden_part, grad_gain_two, grad_shift_two = norm_two_back(grad_normed_two)
    grad_hidden = grad_rows + grad_hidden_part
    grad_scale_one = jnp.sum(grad_hidden * projected, axis=0)
    grad_projected = (grad_hidden * vector_rows[5]).astype(jnp.bfloat16)
    grad_output_bias = jnp.sum(grad_projected.astype(jnp.float32), axis=0)
    grad_output = contract_rows(attended_rows, grad_projected)
    grad_attended = times_transpose(grad_projected, full_output).astype(jnp.bfloat16)
    grad_attended = grad_attended.reshape(image_count, local_len, H, HD)
    grad_by_head = lax.all_to_all(grad_attended, "seq", split_axis=2, concat_axis=1, tiled=True)
    grad_blocks = lax.map(attend_backward, (by_head, grad_by_head, log_total, lengths))
    grad_tok = lax.all_to_all(grad_blocks, "seq", split_axis=1, concat_axis=3, tiled=True)
    grad_joint_rows = grad_tok.reshape(-1, 3 * model_width)
    grad_joint = contract_rows(normed_low, grad_joint_rows)
    joint_sums = jnp.sum(grad_joint_rows.astype(jnp.float32), axis=0)
    grad_normed = times_transpose(grad_joint_rows, full_joint)
    grad_input_part, grad_gain_one, grad_shift_one = norm_one_back(grad_normed)
    input_grad = (grad_hidden + grad_input_part).astype(jnp.bfloat16).reshape(tokens.shape)
    grad_vectors = jnp.stack(
        [
            grad_gain_one,
            grad_shift_one,
            joint_sums[:model_width],
            joint_sums[2 * model_width :],
            grad_output_bias,
            grad_scale_one,
            grad_gain_two,
            grad_shift_two,
            grad_reduce_bias,
            grad_scale_two,
        ],
        axis=0,
    )
    summed_grads = (
        lax.psum_scatter(grad_joint, ("seq", "fsdp"), scatter_dimension=0, tiled=True),
        lax.psum_scatter(grad_output, ("seq", "fsdp"), scatter_dimension=0, tiled=True),
        lax.psum_scatter(grad_expand, ("seq", "fsdp"), scatter_dimension=0, tiled=True),
        lax.psum_scatter(grad_reduce, ("seq", "fsdp"), scatter_dimension=0, tiled=True),
        lax.psum_scatter(grad_vectors, ("seq", "fsdp"), scatter_dimension=1, tiled=True),
        lax.psum_scatter(grad_hidden_bias, ("seq", "fsdp"), scatter_dimension=0, tiled=True),
    )
    owned_joint, owned_output, owned_expand, owned_reduce, owned_vectors, owned_bias = summed_grads
    owned = (owned_joint, owned_output, owned_expand, owned_reduce, owned_vectors, owned_bias)
    shards = (joint_weight, output_weight, expand_weight, reduce_weight, vectors, expand_bias)
    firsts = (first_joint, first_output, first_expand, first_reduce, first_vectors, first_bias)
    seconds = (
        second_joint,
        second_output,
        second_expand,
        second_reduce,
        second_vectors,
        second_bias,
    )
    updates = [
        adam_update(
            shards[index],
            owned[index],
            firsts[index],
            seconds[index],
            STEP_RATES[index],
            DECAY_RATES[index],
        )
        for index in range(6)
    ]
    return (
        block_output,
        input_grad,
        owned[0],
        owned[1],
        owned[2],
        owned[3],
        owned[4],
        owned[5],
        updates[0][0],
        updates[1][0],
        updates[2][0],
        updates[3][0],
        updates[4][0],
        updates[5][0],
        updates[0][1],
        updates[1][1],
        updates[2][1],
        updates[3][1],
        updates[4][1],
        updates[5][1],
        updates[0][2],
        updates[1][2],
        updates[2][2],
        updates[3][2],
        updates[4][2],
        updates[5][2],
    )


def solution(mesh):
    return jax.shard_map(
        body,
        mesh=mesh,
        in_specs=(
            P("fsdp", "seq", None),
            P("fsdp", "seq", None),
            P("fsdp"),
            P(("seq", "fsdp"), None),
            P(("seq", "fsdp"), None),
            P(("seq", "fsdp"), None),
            P(("seq", "fsdp"), None),
            P(None, ("seq", "fsdp")),
            P(("seq", "fsdp")),
            P(("seq", "fsdp"), None),
            P(("seq", "fsdp"), None),
            P(("seq", "fsdp"), None),
            P(("seq", "fsdp"), None),
            P(None, ("seq", "fsdp")),
            P(("seq", "fsdp")),
            P(("seq", "fsdp"), None),
            P(("seq", "fsdp"), None),
            P(("seq", "fsdp"), None),
            P(("seq", "fsdp"), None),
            P(None, ("seq", "fsdp")),
            P(("seq", "fsdp")),
        ),
        out_specs=(
            P("fsdp", "seq", None),
            P("fsdp", "seq", None),
            P(("seq", "fsdp"), None),
            P(("seq", "fsdp"), None),
            P(("seq", "fsdp"), None),
            P(("seq", "fsdp"), None),
            P(None, ("seq", "fsdp")),
            P(("seq", "fsdp")),
            P(("seq", "fsdp"), None),
            P(("seq", "fsdp"), None),
            P(("seq", "fsdp"), None),
            P(("seq", "fsdp"), None),
            P(None, ("seq", "fsdp")),
            P(("seq", "fsdp")),
            P(("seq", "fsdp"), None),
            P(("seq", "fsdp"), None),
            P(("seq", "fsdp"), None),
            P(("seq", "fsdp"), None),
            P(None, ("seq", "fsdp")),
            P(("seq", "fsdp")),
            P(("seq", "fsdp"), None),
            P(("seq", "fsdp"), None),
            P(("seq", "fsdp"), None),
            P(("seq", "fsdp"), None),
            P(None, ("seq", "fsdp")),
            P(("seq", "fsdp")),
        ),
        check_vma=False,
    )
```

profile of v0, /device:TPU:0, one launch (start us, length us, event | category | flops | bytes accessed | tf_op | source)
XLA Modules:
  0.0 1869.3 jit_solution(5718900188525764657)
XLA Ops:
  9.4 72.6 %all-gather = bf16[32,32,10]{1,2,0:T(8,128)(2,1)S(1)} all-gather(bf16[1,32,10]{1,2,0:T(8,128)(2,1)} %bitcast.216), channel_id=1, replica_groups=mesh['seq'=8,'fsdp'=4] {'seq','fsdp'}, dimensions={0}, use_global_device_ids=true | all-gather | bytes 21120 | tf_op jit(solution)/shard_map/all_gather | solution.py:130
  93.9 8.8 reshape.306
  102.6 10.2 copy.80
  118.0 59.7 %all-to-all-done = bf16[3,172,3,16,64]{1,4,2,0,3:T(8,128)(2,1)} async-done(((bf16[3,172,3,16,64]{1,4,2,0,3:T(8,128)(2,1)}), bf16[3,172,3,16,64]{1,4,2,0,3:T(8,128)(2,1)}, u32[]{:S(2)}, u32[]{:S(2)}) %all-to-all-start) | async-done | bytes 3170336 | tf_op jit(solution)/shard_map/all_to_all | solution.py:142
  192.7 74.2 %while.22 = (s32[]{:T(128)}, bf16[3,1376,2,64]{1,3,2,0:T(8,128)(2,1)}, f32[3,2,1376,1]{2,1,3,0:T(2,128)S(1)}, bf16[3,1376,3,2,64]{1,4,3,2,0:T(8,128)(2,1)S(1)}, s32[3]{0:T(128)S(1)}, /*index=5*/s32[]{:T(128)}) while((s32[]{:T(128)}, bf16[3,1376,2,64]{1,3,2,0:T(8,128)(2,1)}, f32[3,2,1376,1]{2,1,3,0:T(2,128)S(1)}, ...), condition=%wide.region_5.6_spmd, body=%wide.region_2.5_spmd.sunk | while | flops 999877312 | bytes 49441980 | solution.py:143
  208.3 9.0 fusion.106
  233.2 9.1 fusion.106
  257.9 9.0 fusion.106
  282.1 67.3 %all-gather.1 = bf16[32,1,128]{2,1,0:T(2,128)(2,1)S(1)} all-gather(bf16[1,1,128]{2,1,0:T(2,128)(2,1)S(1)} %bitcast.227), channel_id=1, replica_groups=mesh['seq'=8,'fsdp'=4] {'seq','fsdp'}, dimensions={0}, use_global_device_ids=true | all-gather | bytes 8448 | tf_op jit(solution)/shard_map/all_gather | solution.py:131
  374.0 28.5 %multiply_convert_fusion.1 = (bf16[516,4096]{1,0:T(8,128)(2,1)}, f32[516,4096]{1,0:T(8,128)}, f32[516,4096]{1,0:T(8,128)}) fusion(f32[4096]{0:T(1024)S(1)} %bitcast.212, bf16[1024,4096]{1,0:T(8,128)(2,1)} %all-gather.11.cloned.1.call-done, f32[516,1024]{1,0:T(8,128)} %copy-done.10, f32[1024]{0:T(1024)S(1)} %bitcast.217, f32[1024]{0:T(1024)S(1)} %bitcast.219, ...), kind=kOutput, calls=%fused_computation.46 | convolution fusion | flops 4470657024 | bytes 31666208 | tf_op jit(solution)/shard_map/dot_general | solution.py:153
  402.6 15.1 convert_reduce_fusion.1
  417.7 11.9 multiply_reduce_fusion.3
  429.7 9.1 fusion.63
  458.8 21.0 %all-to-all-done.2 = bf16[3,172,16,64]{1,3,0,2:T(8,128)(2,1)} async-done(((bf16[3,172,16,64]{1,3,0,2:T(8,128)(2,1)}), bf16[3,172,16,64]{1,3,0,2:T(8,128)(2,1)}, u32[]{:S(2)}, u32[]{:S(2)}) %all-to-all-start.2) | async-done | bytes 1056800 | tf_op jit(solution)/shard_map/all_to_all | solution.py:193
  487.1 86.6 %while.23 = (s32[]{:T(128)}, bf16[3,1376,3,2,64]{1,4,3,2,0:T(8,128)(2,1)}, bf16[3,1376,3,2,64]{1,4,3,2,0:T(8,128)(2,1)S(1)}, s32[3]{0:T(128)S(1)}, f32[3,2,1376,...) while((s32[]{:T(128)}, bf16[3,1376,3,2,64]{1,4,3,2,0:T(8,128)(2,1)}, ...), condition=%wide.region_12.13_spmd, body=%wide.region_10.12_spmd.sunk | while | flops 2461651456 | bytes 187365392 | solution.py:194
  491.8 8.5 multiply_reduce_fusion.10
  549.5 8.5 multiply_reduce_fusion.10
  573.7 17.5 copy.86
  591.3 10.0 reshape.329
  606.8 36.4 %all-to-all-done.3 = bf16[8,2,99072]{2,1,0:T(2,128)(2,1)S(1)} async-done(((bf16[8,2,99072]{2,1,0:T(2,128)(2,1)}), bf16[8,2,99072]{2,1,0:T(2,128)(2,1)S(1)}, u32[]{:S(2)}, u32[]{:S(2)}) %all-to-all-start.3) | async-done | bytes 3170336 | tf_op jit(solution)/shard_map/all_to_all | solution.py:195
  643.1 8.9 reshape.330
  667.0 14.6 reshape.310
  681.9 8.9 multiply_reduce_fusion.5
  701.2 9.9 fusion.69
  711.9 13.1 fusion.54
  725.7 12.8 fusion.52
  740.8 37.4 %all-reduce = f32[4096]{0:T(1024)S(1)} all-reduce(f32[4096]{0:T(1024)S(1)} %copy-done.52), channel_id=7, replica_groups=mesh['seq'=8,'fsdp'=4] {'seq','fsdp'}, use_global_device_ids=true, to_apply=%region_30.31.clone | all-reduce | flops 4096 | bytes 32768
  782.8 41.9 %reduce-scatter.16.cloned.1.call-done = f32[32,10]{1,0:T(8,128)} async-done(((f32[1024,10]{1,0:T(8,128)}), f32[32,10]{1,0:T(8,128)}) %reduce-scatter.16.cloned.1.call-update) | async-done | bytes 1296
  826.2 146.4 %reduce-scatter.10.cloned.1.call-done = f32[32,1024]{1,0:T(8,128)} async-done(((f32[1024,1024]{1,0:T(8,128)}), f32[32,1024]{1,0:T(8,128)}) %reduce-scatter.10.cloned.1.call-update) | async-done | bytes 131088 | tf_op jit(solution)/shard_map/reduce_scatter | solution.py:219
  974.3 158.5 %reduce-scatter.8.cloned.1.call-done = f32[32,3072]{1,0:T(8,128)} async-done(((f32[1024,3072]{1,0:T(8,128)}), f32[32,3072]{1,0:T(8,128)}) %reduce-scatter.8.cloned.1.call-update) | async-done | bytes 393232 | tf_op jit(solution)/shard_map/reduce_scatter | solution.py:218
  1135.1 360.2 %reduce-scatter.12.cloned.1.call-done = f32[32,4096]{1,0:T(8,128)} async-done(((f32[1024,4096]{1,0:T(8,128)}), f32[32,4096]{1,0:T(8,128)}) %reduce-scatter.12.cloned.1.call-update) | async-done | bytes 524304 | tf_op jit(solution)/shard_map/reduce_scatter | solution.py:220
  1497.7 362.4 %reduce-scatter.14.cloned.1.call-done = f32[128,1024]{1,0:T(8,128)} async-done(((f32[4096,1024]{1,0:T(8,128)}), f32[128,1024]{1,0:T(8,128)}) %reduce-scatter.14.cloned.1.call-update) | async-done | bytes 524304 | tf_op jit(solution)/shard_map/reduce_scatter | solution.py:221
  (302 shorter events, 266.9 us)
Async XLA Ops:
  7.2 76.3 %copy-start.5 = (bf16[3,172,1024]{2,1,0:T(8,128)(2,1)S(1)}, bf16[3,172,1024]{2,1,0:T(8,128)(2,1)}, u32[]{:S(2)}) copy-start(bf16[3,172,1024]{2,1,0:T(8,128)(2,1)} %param.25) | copy-start | bytes 3170308
  7.2 78.5 %all-gather.7.cloned.1.call-start = ((), (), s32[]{:S(2)}) async-start(), calls=%async_computation.9 | async-start | bytes 6488064 | tf_op jit(solution)/shard_map/all_gather | solution.py:126
  7.9 359.0 %all-gather.9.cloned.1.call-start = ((), (), s32[]{:S(2)}) async-start(), calls=%async_computation.10 | async-start | bytes 2162688 | tf_op jit(solution)/shard_map/all_gather | solution.py:127
  8.7 365.3 %all-gather.11.cloned.1.call-start = ((), (), s32[]{:S(2)}) async-start(), calls=%async_computation.11 | async-start | bytes 8650752 | tf_op jit(solution)/shard_map/all_gather | solution.py:128
  112.8 64.9 %all-to-all-start = ((bf16[3,172,3,16,64]{1,4,2,0,3:T(8,128)(2,1)}), bf16[3,172,3,16,64]{1,4,2,0,3:T(8,128)(2,1)}, u32[]{:S(2)}, u32[]{:S(2)}) async-start(bf16[3,172,3,16,64]{1,4,2,0,3:T(8,128)(2,1)} %copy.80), calls=%async_computation | async-start | bytes 9437184 | tf_op jit(solution)/shard_map/all_to_all | solution.py:142
  117.4 285.2 %all-gather.13.cloned.1.call-start = ((), (), s32[]{:S(2)}) async-start(), calls=%async_computation.12 | async-start | bytes 8650752 | tf_op jit(solution)/shard_map/all_gather | solution.py:129
  277.9 74.3 %all-to-all-start.1 = ((bf16[8,2,33024]{2,1,0:T(2,128)(2,1)}), bf16[8,2,33024]{2,1,0:T(2,128)(2,1)}, u32[]{:S(2)}, u32[]{:S(2)}) async-start(bf16[8,2,33024]{2,1,0:T(2,128)(2,1)} %reshape.327), calls=%async_computation.1 | async-start | bytes 2113536 | tf_op jit(solution)/shard_map/all_to_all | solution.py:144
  349.6 89.3 %copy-start.45 = (f32[516]{0:T(1024)}, f32[516]{0:T(1024)S(1)}, u32[]{:S(2)}) copy-start(f32[516]{0:T(1024)S(1)} %reshape.318) | copy-start | bytes 6196
  372.2 57.4 %copy-start.47 = (f32[516]{0:T(1024)}, f32[516]{0:T(1024)S(1)}, u32[]{:S(2)}) copy-start(f32[516]{0:T(1024)S(1)} %broadcast_multiply_fusion) | copy-start | bytes 6196
  374.0 55.7 %copy-start.64 = (f32[516]{0:T(1024)}, f32[516]{0:T(1024)S(1)}, u32[]{:S(2)}) copy-start(f32[516]{0:T(1024)S(1)} %fusion.49) | copy-start | bytes 6196
  454.3 25.5 %all-to-all-start.2 = ((bf16[3,172,16,64]{1,3,0,2:T(8,128)(2,1)}), bf16[3,172,16,64]{1,3,0,2:T(8,128)(2,1)}, u32[]{:S(2)}, u32[]{:S(2)}) async-start(bf16[3,172,16,64]{1,3,0,2:T(8,128)(2,1)} %copy.84), calls=%async_computation.2 | async-start | bytes 3145728 | tf_op jit(solution)/shard_map/all_to_all | solution.py:193
  601.3 41.8 %all-to-all-start.3 = ((bf16[8,2,99072]{2,1,0:T(2,128)(2,1)}), bf16[8,2,99072]{2,1,0:T(2,128)(2,1)S(1)}, u32[]{:S(2)}, u32[]{:S(2)}) async-start(bf16[8,2,99072]{2,1,0:T(2,128)(2,1)} %reshape.329), calls=%async_computation.3 | async-start | bytes 6340608 | tf_op jit(solution)/shard_map/all_to_all | solution.py:195
  605.1 219.6 %reduce-scatter.16.cloned.1.call-start = ((), (), s32[]{:S(2)}) async-start(), calls=%async_computation.17 | async-start | bytes 540672
  691.9 280.7 %reduce-scatter.10.cloned.1.call-start = ((), (), s32[]{:S(2)}) async-start(), calls=%async_computation.14 | async-start | bytes 4325376 | tf_op jit(solution)/shard_map/reduce_scatter | solution.py:219
  697.1 435.8 %reduce-scatter.8.cloned.1.call-start = ((), (), s32[]{:S(2)}) async-start(), calls=%async_computation.13 | async-start | bytes 12976128 | tf_op jit(solution)/shard_map/reduce_scatter | solution.py:218
  711.2 784.1 %reduce-scatter.12.cloned.1.call-start = ((), (), s32[]{:S(2)}) async-start(), calls=%async_computation.15 | async-start | bytes 17301504 | tf_op jit(solution)/shard_map/reduce_scatter | solution.py:220
  725.0 1135.1 %reduce-scatter.14.cloned.1.call-start = ((), (), s32[]{:S(2)}) async-start(), calls=%async_computation.16 | async-start | bytes 17301504 | tf_op jit(solution)/shard_map/reduce_scatter | solution.py:221
  781.6 44.0 %copy-start.53 = (bf16[10,32]{1,0:T(8,128)(2,1)S(1)}, bf16[10,32]{1,0:T(8,128)(2,1)}, u32[]{:S(2)}) copy-start(bf16[10,32]{1,0:T(8,128)(2,1)} %param.32) | copy-start | bytes 1924
  781.6 44.0 %copy-start.58 = (f32[10,32]{1,0:T(8,128)S(1)}, f32[10,32]{1,0:T(8,128)}, u32[]{:S(2)}) copy-start(f32[10,32]{1,0:T(8,128)} %param.38) | copy-start | bytes 3844
  781.6 191.0 %copy-start.25 = (bf16[32,1024]{1,0:T(8,128)(2,1)S(1)}, bf16[32,1024]{1,0:T(8,128)(2,1)}, u32[]{:S(2)}) copy-start(bf16[32,1024]{1,0:T(8,128)(2,1)} %param.29) | copy-start | bytes 196612
  781.6 191.0 %copy-start.26 = (f32[32,1024]{1,0:T(8,128)S(1)}, f32[32,1024]{1,0:T(8,128)}, u32[]{:S(2)}) copy-start(f32[32,1024]{1,0:T(8,128)} %param.35) | copy-start | bytes 393220
  781.6 191.0 %copy-start.27 = (f32[32,1024]{1,0:T(8,128)S(1)}, f32[32,1024]{1,0:T(8,128)}, u32[]{:S(2)}) copy-start(f32[32,1024]{1,0:T(8,128)} %param.41) | copy-start | bytes 393220
  781.6 351.2 %copy-start.18 = (bf16[32,3072]{1,0:T(8,128)(2,1)S(1)}, bf16[32,3072]{1,0:T(8,128)(2,1)}, u32[]{:S(2)}) copy-start(bf16[32,3072]{1,0:T(8,128)(2,1)} %param.28) | copy-start | bytes 589828
  781.6 351.2 %copy-start.23 = (f32[32,3072]{1,0:T(8,128)S(1)}, f32[32,3072]{1,0:T(8,128)}, u32[]{:S(2)}) copy-start(f32[32,3072]{1,0:T(8,128)} %param.34) | copy-start | bytes 1179652
  781.7 351.2 %copy-start.24 = (f32[32,3072]{1,0:T(8,128)S(1)}, f32[32,3072]{1,0:T(8,128)}, u32[]{:S(2)}) copy-start(f32[32,3072]{1,0:T(8,128)} %param.40) | copy-start | bytes 1179652
  782.8 712.4 %copy-start.16 = (bf16[32,4096]{1,0:T(8,128)(2,1)S(1)}, bf16[32,4096]{1,0:T(8,128)(2,1)}, u32[]{:S(2)}) copy-start(bf16[32,4096]{1,0:T(8,128)(2,1)} %param.30) | copy-start | bytes 786436
  782.8 712.4 %copy-start.19 = (f32[32,4096]{1,0:T(8,128)S(1)}, f32[32,4096]{1,0:T(8,128)}, u32[]{:S(2)}) copy-start(f32[32,4096]{1,0:T(8,128)} %param.36) | copy-start | bytes 1572868
  782.8 712.4 %copy-start.20 = (f32[32,4096]{1,0:T(8,128)S(1)}, f32[32,4096]{1,0:T(8,128)}, u32[]{:S(2)}) copy-start(f32[32,4096]{1,0:T(8,128)} %param.42) | copy-start | bytes 1572868
  825.5 672.1 %copy-start.36 = (f32[10,32]{1,0:T(8,128)}, f32[10,32]{1,0:T(8,128)S(1)}, u32[]{:S(2)}) copy-start(f32[10,32]{1,0:T(8,128)S(1)} %copy.93) | copy-start | bytes 3844
  1135.1 725.0 %copy-start.17 = (bf16[128,1024]{1,0:T(8,128)(2,1)S(1)}, bf16[128,1024]{1,0:T(8,128)(2,1)}, u32[]{:S(2)}) copy-start(bf16[128,1024]{1,0:T(8,128)(2,1)} %param.31) | copy-start | bytes 786436
  1135.1 725.0 %copy-start.21 = (f32[128,1024]{1,0:T(8,128)S(1)}, f32[128,1024]{1,0:T(8,128)}, u32[]{:S(2)}) copy-start(f32[128,1024]{1,0:T(8,128)} %param.37) | copy-start | bytes 1572868
  1135.1 725.0 %copy-start.22 = (f32[128,1024]{1,0:T(8,128)S(1)}, f32[128,1024]{1,0:T(8,128)}, u32[]{:S(2)}) copy-start(f32[128,1024]{1,0:T(8,128)} %param.43) | copy-start | bytes 1572868
  (61 other events, 574.7 us)
Sparse Core Ops, SparseCore 0:
  10.9 72.2 all-gather.6
  86.1 69.8 all-gather.8
  158.9 76.6 all-gather.10
  238.4 84.8 all-gather.12
  692.1 132.6 reduce-scatter.15
  827.4 145.1 reduce-scatter.9
  979.2 153.6 reduce-scatter.7
  1135.7 359.4 reduce-scatter.11
  1498.1 361.9 reduce-scatter.13
where the time goes:
time: 1880 us; the launch traced here: 1870 us
  waiting for transfers between devices  1190 us (63%)
  matrix products  228 us (12%)
  blocking collectives  177 us (9%)
  local copies, waits for them, and re-layouts  165 us (9%)
  other arithmetic  77.4 us (4%)
    reduce_scatter x1, waiting for transfers between devices, body(): lax.psum_scatter(grad_reduce, ('seq', 'fsdp'), scatter_dimension=0, tiled...  362 us
    reduce_scatter x1, waiting for transfers between devices, body(): lax.psum_scatter(grad_expand, ('seq', 'fsdp'), scatter_dimension=0, tiled...  360 us
    reduce_scatter x1, waiting for transfers between devices, body(): lax.psum_scatter(grad_joint, ('seq', 'fsdp'), scatter_dimension=0, tiled=...  159 us
    reduce_scatter x1, waiting for transfers between devices, body(): lax.psum_scatter(grad_output, ('seq', 'fsdp'), scatter_dimension=0, tiled...  146 us
    all_gather x1, blocking collectives, body(): lax.all_gather(vectors, ('seq', 'fsdp'), axis=1, tiled=True)  72.6 us
    all_gather x1, blocking collectives, body(): lax.all_gather(expand_bias, ('seq', 'fsdp'), axis=0, tiled=True)  67.3 us
    all_to_all x1, waiting for transfers between devices, body(): lax.all_to_all(joint_low, 'seq', split_axis=3, concat_axis=1, tiled=True)  59.7 us
    dot_general x6, matrix products, head_scores(): jnp.einsum('qhd,khd->hqk', queries, key_rows, preferred_element_type=jnp....  46.1 us
  transfers between devices with their start and end apart: 13, of which 8 were waited for; matrix products, arithmetic and copies ran while one was open for 13% of the time, Pallas kernels for 0%

commit v1 on v0

v1 whole, which is shorter than its diff:
```python
import jax
import jax.numpy as jnp
from jax import lax
from jax.experimental import pallas as pl
from jax.experimental.pallas import tpu as pltpu
from jax.sharding import PartitionSpec as P

H = 16
HD = 64
ADAM_STEP = 2

EPS_NORM = 1e-06
MASK_LOW = -1e30
BETA_ONE = 0.9
BETA_TWO = 0.999
EPS_ADAM = 1e-08
STEP_RATES = (0.006, 0.05, 0.006, 0.004, 0.15, 0.02)
DECAY_RATES = (0.04, 0.04, 0.04, 0.04, 0.0, 0.0)
BOTH = ("seq", "fsdp")
F32 = jnp.float32
BF16 = jnp.bfloat16


def norm_apply(features, gain_row, shift_row):
    average = jnp.mean(features, axis=-1, keepdims=True)
    centered = features - average
    spread = jnp.mean(centered * centered, axis=-1, keepdims=True)
    return centered * lax.rsqrt(spread + EPS_NORM) * gain_row + shift_row


def gelu_parts(values):
    cdf = 0.5 * (1.0 + lax.erf(values * 0.7071067811865476))
    slope = cdf + values * (0.3989422804014327 * jnp.exp(-0.5 * values * values))
    return values * cdf, slope


def dot(left, right):
    return jnp.dot(left, right, preferred_element_type=F32)


def dot_rows(left, right):
    return lax.dot_general(left, right, (((0,), (0,)), ((), ())), preferred_element_type=F32)


def dot_t(left, right):
    return lax.dot_general(left, right, (((1,), (1,)), ((), ())), preferred_element_type=F32)


def pick(stack, index):
    return lax.dynamic_index_in_dim(stack, index, 0, keepdims=False)


def place(stack, piece, index):
    return lax.dynamic_update_index_in_dim(stack, piece, index, 0)


def shift_pairs(count, step):
    return [(i, (i + step) % count) for i in range(count)]


def gather_ring(piece, axis, count):
    me = lax.axis_index(axis)
    out = place(jnp.zeros((count,) + piece.shape, piece.dtype), piece, me)
    for step in range(1, count):
        got = lax.ppermute(piece, axis, shift_pairs(count, step))
        out = place(out, got, (me - step) % count)
    return out


def scatter_sum(parts, axis, count):
    me = lax.axis_index(axis)
    total = pick(parts, me)
    for step in range(1, count):
        sent = pick(parts, (me + step) % count)
        total = total + lax.ppermute(sent, axis, shift_pairs(count, step))
    return total


def gather_plane(piece, count):
    if count != 8:
        return lax.all_gather(piece, "seq", axis=0)
    me = lax.axis_index("seq")
    first = jnp.where(me % 2 == 0, 2, 4)
    second = 6 - first
    pairs_one = [(i, i ^ (2 if i % 2 == 0 else 4)) for i in range(8)]
    pairs_two = [(i, i ^ (4 if i % 2 == 0 else 2)) for i in range(8)]
    pairs_core = [(i, i ^ 1) for i in range(8)]
    one = lax.ppermute(piece, "seq", pairs_one)
    two = lax.ppermute(piece, "seq", pairs_two)
    three = lax.ppermute(one, "seq", pairs_two)
    mine = ((piece, me), (one, me ^ first), (two, me ^ second), (three, me ^ 6))
    theirs = (me ^ 1, me ^ 1 ^ second, me ^ 1 ^ first, me ^ 7)
    out = jnp.zeros((8,) + piece.shape, piece.dtype)
    for (block, index), other in zip(mine, theirs):
        out = place(out, block, index)
        out = place(out, lax.ppermute(block, "seq", pairs_core), other)
    return out


def head_lanes(shape, head):
    lane = lax.broadcasted_iota(jnp.int32, shape, len(shape) - 1)
    inside = (lane >= head * HD) & (lane < (head + 1) * HD)
    spare = lane == (HD if head == 0 else 0)
    return inside, spare


def attend_fwd_kernel(lens_ref, pos_ref, joint_ref, out_ref, q_scr, k_scr, v_scr, o_scr, *, heads, block):
    rows, width = o_scr.shape
    image = pl.program_id(0)

    def part(index):
        return joint_ref[:, 0, :, index * width : (index + 1) * width].reshape(rows, width)

    queries = part(0).astype(F32) * 0.125
    key_rows = part(1).astype(F32)
    v_scr[...] = part(2)
    bias = jnp.where(pos_ref[...] < lens_ref[image], 0.0, MASK_LOW)
    for head in range(heads):
        inside, spare = head_lanes((rows, width), head)
        q_scr[head] = jnp.where(inside, queries, jnp.where(spare, 1.0, 0.0)).astype(BF16)
        k_scr[head] = jnp.where(inside, key_rows, jnp.where(spare, bias, 0.0)).astype(BF16)

    def step(index, carry):
        start = pl.multiple_of(index * block, 16)
        value = None
        for head in range(heads):
            scores = dot_t(q_scr[head, pl.ds(start, block), :], k_scr[head])
            highest = jnp.max(scores, axis=1, keepdims=True)
            exponent = jnp.exp(scores - highest)
            inverse = 1.0 / jnp.sum(exponent, axis=1, keepdims=True)
            probs = (exponent * inverse).astype(BF16)
            result = dot(probs, v_scr[...])
            if head == 0:
                value = result
            else:
                inside, _ = head_lanes((block, width), head)
                value = jnp.where(inside, result, value)
        o_scr[pl.ds(start, block), :] = value
        return carry

    lax.fori_loop(0, rows // block, step, 0)
    out_ref[:, 0] = o_scr[...].astype(BF16).reshape(out_ref.shape[0], out_ref.shape[2], width)


def attend_bwd_kernel(
    lens_ref, pos_ref, joint_ref, grad_ref, out_ref, q_scr, k_scr, v_scr, g_scr, dq_scr, dk_scr, dv_scr, *, heads, block
):
    rows, width = v_scr.shape
    image = pl.program_id(0)

    def part(index):
        return joint_ref[:, 0, :, index * width : (index + 1) * width].reshape(rows, width)

    queries = part(0).astype(F32) * 0.125
    key_rows = part(1).astype(F32)
    grads = grad_ref[:, 0].reshape(rows, width).astype(F32)
    v_scr[...] = part(2)
    bias = jnp.where(pos_ref[...] < lens_ref[image], 0.0, MASK_LOW)
    for head in range(heads):
        inside, spare = head_lanes((rows, width), head)
        q_scr[head] = jnp.where(inside, queries, 0.0).astype(BF16)
        g_scr[head] = jnp.where(inside, grads, 0.0).astype(BF16)
        k_scr[head] = jnp.where(inside, key_rows, jnp.where(spare, bias, 0.0)).astype(BF16)
    dk_scr[...] = jnp.zeros_like(dk_scr)
    dv_scr[...] = jnp.zeros_like(dv_scr)

    def tile(start, size):
        dq = None
        dk = None
        dv = None
        for head in range(heads):
            _, spare = head_lanes((size, width), head)
            q_tile = q_scr[head, pl.ds(start, size), :]
            g_tile = g_scr[head, pl.ds(start, size), :]
            q_mask = jnp.where(spare, 1.0, q_tile.astype(F32)).astype(BF16)
            scores = dot_t(k_scr[head], q_mask)
            highest = jnp.max(scores, axis=0, keepdims=True)
            exponent = jnp.exp(scores - highest)
            probs = exponent * (1.0 / jnp.sum(exponent, axis=0, keepdims=True))
            grad_probs = dot_t(v_scr[...], g_tile)
            inner = jnp.sum(probs * grad_probs, axis=0, keepdims=True)
            grad_scores = (probs * (grad_probs - inner)).astype(BF16)
            dv_h = dot(probs.astype(BF16), g_tile)
            dk_h = dot(grad_scores, q_tile)
            dq_h = dot_rows(grad_scores, k_scr[head])
            dq = dq_h if dq is None else dq + dq_h
            dk = dk_h if dk is None else dk + dk_h
            dv = dv_h if dv is None else dv + dv_h
        dq_scr[pl.ds(start, size), :] = dq * 0.125
        dk_scr[...] += dk
        dv_scr[...] += dv

    def step(index, carry):
        tile(pl.multiple_of(index * block, 16), block)
        return carry

    whole = rows // block
    lax.fori_loop(0, whole, step, 0)
    if rows % block:
        tile(whole * block, rows % block)
    for index, grad in enumerate((dq_scr, dk_scr, dv_scr)):
        out_ref[:, 0, :, index * width : (index + 1) * width] = (
            grad[...].astype(BF16).reshape(out_ref.shape[0], out_ref.shape[2], width)
        )


def attend_specs(shape, width):
    parts, _, length, _ = shape
    rows = parts * length
    pos_spec = pl.BlockSpec((rows, width), lambda i, lens: (0, 0))

    def wide(count):
        return pl.BlockSpec((parts, 1, length, count * width), lambda i, lens: (0, i, 0, 0))

    return rows, pos_spec, wide


def attend_forward(joint, lengths, positions, heads, width):
    rows, pos_spec, wide = attend_specs(joint.shape, width)
    images = joint.shape[1]
    block = rows // 4

    def kernel(*refs):
        attend_fwd_kernel(*refs, heads=heads, block=block)

    return pl.pallas_call(
        kernel,
        out_shape=jax.ShapeDtypeStruct(joint.shape[:3] + (width,), BF16),
        grid_spec=pltpu.PrefetchScalarGridSpec(
            num_scalar_prefetch=1,
            grid=(images,),
            in_specs=[pos_spec, wide(3)],
            out_specs=wide(1),
            scratch_shapes=[
                pltpu.VMEM((heads, rows, width), BF16),
                pltpu.VMEM((heads, rows, width), BF16),
                pltpu.VMEM((rows, width), BF16),
                pltpu.VMEM((rows, width), F32),
            ],
        ),
        name="attend_forward",
    )(lengths, positions, joint)


def attend_backward(joint, grads, lengths, positions, heads, width):
    rows, pos_spec, wide = attend_specs(joint.shape, width)
    images = joint.shape[1]

    def kernel(*refs):
        attend_bwd_kernel(*refs, heads=heads, block=256)

    return pl.pallas_call(
        kernel,
        out_shape=jax.ShapeDtypeStruct(joint.shape, BF16),
        grid_spec=pltpu.PrefetchScalarGridSpec(
            num_scalar_prefetch=1,
            grid=(images,),
            in_specs=[pos_spec, wide(3), wide(1)],
            out_specs=wide(3),
            scratch_shapes=[
                pltpu.VMEM((heads, rows, width), BF16),
                pltpu.VMEM((heads, rows, width), BF16),
                pltpu.VMEM((rows, width), BF16),
                pltpu.VMEM((heads, rows, width), BF16),
                pltpu.VMEM((rows, width), F32),
                pltpu.VMEM((rows, width), F32),
                pltpu.VMEM((rows, width), F32),
            ],
        ),
        name="attend_backward",
    )(lengths, positions, joint, grads)


def adam_update(weight, gradient, moment_one, moment_two, step_rate, decay_rate):
    mean_new = BETA_ONE * moment_one + (1.0 - BETA_ONE) * gradient
    square_new = BETA_TWO * moment_two + (1.0 - BETA_TWO) * gradient * gradient
    mean_hat = mean_new / (1.0 - BETA_ONE**ADAM_STEP)
    square_hat = square_new / (1.0 - BETA_TWO**ADAM_STEP)
    weight_f = weight.astype(F32)
    updated = weight_f - step_rate * (
        mean_hat / (jnp.sqrt(square_hat) + EPS_ADAM) + decay_rate * weight_f
    )
    return (updated, mean_new, square_new)


def make_body(ns, nf):
    def body(
        tokens,
        cotangent,
        lengths,
        joint_weight,
        output_weight,
        expand_weight,
        reduce_weight,
        vectors,
        expand_bias,
        *moments,
    ):
        images, local_len, width = tokens.shape
        pad_len = -(-local_len // 16) * 16
        rows = images * pad_len
        heads = H // ns
        own = heads * HD
        lanes = max(own, 128)
        hidden = expand_weight.shape[1]
        slice_ff = hidden // ns
        seq = lax.axis_index("seq")

        def padded(array):
            array = jnp.pad(array, ((0, 0), (0, pad_len - local_len), (0, 0)))
            return array.reshape(rows, width)

        def unpadded(array):
            return array.reshape(images, pad_len, width)[:, :local_len]

        vector_rows = lax.all_gather(vectors, BOTH, axis=1, tiled=True).astype(F32)
        full_bias = lax.all_gather(expand_bias, BOTH, axis=0, tiled=True).astype(F32)

        features = padded(tokens).astype(F32)
        normed, norm_one_back = jax.vjp(norm_apply, features, vector_rows[0], vector_rows[1])
        normed_low = normed.astype(BF16)
        normed_all = gather_plane(normed_low, ns).reshape(ns * rows, width)

        own_rows = joint_weight.shape[0]
        pieces = joint_weight.reshape(own_rows, 3, ns, own).transpose(2, 0, 1, 3)
        pieces = lax.all_to_all(pieces, "seq", split_axis=0, concat_axis=0, tiled=True)
        pieces = gather_ring(pieces, "fsdp", nf)
        joint_own = pieces.transpose(1, 0, 2, 3, 4).reshape(width, 3, own)
        bias_own = lax.dynamic_slice_in_dim(vector_rows[2:4], seq * own, own, axis=1)
        bias_own = jnp.stack([bias_own[0], jnp.zeros_like(bias_own[0]), bias_own[1]])
        if lanes > own:
            joint_own = jnp.pad(joint_own, ((0, 0), (0, 0), (0, lanes - own)))
            bias_own = jnp.pad(bias_own, ((0, 0), (0, lanes - own)))
        joint = dot(normed_all, joint_own.reshape(width, 3 * lanes)) + bias_own.reshape(-1)
        joint = joint.astype(BF16).reshape(ns, images, pad_len, 3 * lanes)

        slot = jnp.arange(pad_len)
        live = (slot[None, :] < local_len) & (seq * local_len + slot[None, :] < lengths[:, None])
        grad_rows = padded(cotangent).astype(F32) * live.astype(F32).reshape(rows, 1)
        grad_reduced = (grad_rows * vector_rows[9]).astype(BF16)

        full_output = lax.all_gather(output_weight, BOTH, axis=0, tiled=True)
        full_expand = lax.all_gather(expand_weight, BOTH, axis=0, tiled=True)
        full_reduce = lax.all_gather(reduce_weight, BOTH, axis=0, tiled=True)
        grad_reduced_all = lax.all_gather(grad_reduced, "seq", axis=0, tiled=True)

        index = jnp.arange(ns * pad_len)
        position = jnp.where(
            index % pad_len < local_len, (index // pad_len) * local_len + index % pad_len, 1 << 30
        ).astype(jnp.int32)
        positions = jnp.broadcast_to(position[:, None], (ns * pad_len, lanes))
        attended = attend_forward(joint, lengths, positions, heads, lanes)
        attended_own = attended.reshape(ns, rows, lanes)[:, :, :own]
        attended_tok = lax.all_to_all(attended_own, "seq", split_axis=0, concat_axis=0, tiled=True)
        attended_rows = attended_tok.transpose(1, 0, 2).reshape(rows, width)

        projected = dot(attended_rows, full_output) + vector_rows[4]
        hidden_one = features + vector_rows[5] * projected
        normed_two, norm_two_back = jax.vjp(norm_apply, hidden_one, vector_rows[6], vector_rows[7])
        normed_two_low = normed_two.astype(BF16)
        normed_two_all = lax.all_gather(normed_two_low, "seq", axis=0, tiled=True)
        expanded = dot(normed_two_low, full_expand) + full_bias
        activated, slope = gelu_parts(expanded)
        reduced = dot(activated.astype(BF16), full_reduce) + vector_rows[8]
        block_output = unpadded((hidden_one + vector_rows[9] * reduced).astype(BF16))

        grad_scale_two = jnp.sum(grad_rows * reduced, axis=0)
        grad_reduce_bias = jnp.sum(grad_reduced.astype(F32), axis=0)
        grad_expanded = (dot_t(grad_reduced, full_reduce) * slope).astype(BF16)
        grad_normed_two = dot_t(grad_expanded, full_expand)
        grad_hidden_part, grad_gain_two, grad_shift_two = norm_two_back(grad_normed_two)
        grad_hidden = grad_rows + grad_hidden_part
        grad_scale_one = jnp.sum(grad_hidden * projected, axis=0)
        grad_projected = (grad_hidden * vector_rows[5]).astype(BF16)
        grad_output_bias = jnp.sum(grad_projected.astype(F32), axis=0)
        grad_attended = dot_t(grad_projected, full_output).astype(BF16)
        grad_attended = grad_attended.reshape(rows, ns, own).transpose(1, 0, 2)
        grad_heads = lax.all_to_all(grad_attended, "seq", split_axis=0, concat_axis=0, tiled=True)
        grad_projected_all = lax.all_gather(grad_projected, "seq", axis=0, tiled=True)
        if lanes > own:
            grad_heads = jnp.pad(grad_heads, ((0, 0), (0, 0), (0, lanes - own)))
        grad_heads = grad_heads.reshape(ns, images, pad_len, lanes)

        expand_own = lax.dynamic_slice_in_dim(full_expand, seq * slice_ff, slice_ff, axis=1)
        reduce_own = lax.dynamic_slice_in_dim(full_reduce, seq * slice_ff, slice_ff, axis=0)
        ff_bias_own = lax.dynamic_slice_in_dim(full_bias, seq * slice_ff, slice_ff, axis=0)
        expanded_own = dot(normed_two_all, expand_own) + ff_bias_own
        activated_own, slope_own = gelu_parts(expanded_own)
        grad_expanded_own = (dot_t(grad_reduced_all, reduce_own) * slope_own).astype(BF16)
        part_reduce = dot_rows(activated_own.astype(BF16), grad_reduced_all)
        part_expand = dot_rows(normed_two_all, grad_expanded_own)
        part_bias = jnp.sum(grad_expanded_own.astype(F32), axis=0)
        own_reduce = scatter_sum(part_reduce.reshape(nf, -1, width), "fsdp", nf)
        own_expand = scatter_sum(
            part_expand.reshape(ns, nf, own_rows, slice_ff).transpose(1, 0, 2, 3), "fsdp", nf
        )
        own_expand = lax.all_to_all(own_expand, "seq", split_axis=0, concat_axis=0, tiled=True)
        own_expand = own_expand.transpose(1, 0, 2).reshape(own_rows, hidden)
        own_bias = scatter_sum(part_bias.reshape(nf, -1), "fsdp", nf)

        grad_joint = attend_backward(joint, grad_heads, lengths, positions, heads, lanes)
        part_output = dot_rows(attended_own.reshape(ns * rows, own), grad_projected_all)
        own_output = scatter_sum(part_output.reshape(nf, -1, width), "fsdp", nf)
        grad_joint_own = grad_joint.reshape(ns * rows, 3, lanes)[:, :, :own].reshape(ns, rows, 3 * own)
        grad_joint_flat = grad_joint_own.reshape(ns * rows, 3 * own)
        part_joint = dot_rows(normed_all, grad_joint_flat)
        joint_sums = jnp.sum(grad_joint_flat.astype(F32), axis=0)
        own_joint = scatter_sum(
            part_joint.reshape(ns, nf, own_rows, 3 * own).transpose(1, 0, 2, 3), "fsdp", nf
        )
        own_joint = lax.all_to_all(own_joint, "seq", split_axis=0, concat_axis=0, tiled=True)
        own_joint = own_joint.reshape(ns, own_rows, 3, own).transpose(1, 2, 0, 3).reshape(own_rows, 3 * width)

        full_joint = lax.all_gather(joint_weight, BOTH, axis=0, tiled=True)
        grad_tok = lax.all_to_all(grad_joint_own, "seq", split_axis=0, concat_axis=0, tiled=True)
        grad_tok = grad_tok.reshape(ns, rows, 3, own).transpose(1, 2, 0, 3).reshape(rows, 3 * width)
        grad_normed = dot_t(grad_tok, full_joint)
        grad_input_part, grad_gain_one, grad_shift_one = norm_one_back(grad_normed)
        input_grad = unpadded((grad_hidden + grad_input_part).astype(BF16))

        token_sums = jnp.stack(
            [
                grad_gain_one,
                grad_shift_one,
                grad_output_bias,
                grad_scale_one,
                grad_gain_two,
                grad_shift_two,
                grad_reduce_bias,
                grad_scale_two,
            ]
        )
        token_sums = token_sums.reshape(8, ns, own).transpose(1, 0, 2)
        plane_sums = pick(token_sums, seq)
        for step in range(1, ns):
            sent = pick(token_sums, (seq + step) % ns)
            plane_sums = plane_sums + lax.ppermute(sent, "seq", shift_pairs(ns, step))
        plane_sums = jnp.concatenate(
            [plane_sums[:2], joint_sums[None, :own], joint_sums[None, 2 * own :], plane_sums[2:]]
        )
        own_vectors = scatter_sum(plane_sums.reshape(10, nf, -1).transpose(1, 0, 2), "fsdp", nf)

        owned = (own_joint, own_output, own_expand, own_reduce, own_vectors, own_bias)
        shards = (joint_weight, output_weight, expand_weight, reduce_weight, vectors, expand_bias)
        updates = [
            adam_update(
                shards[i], owned[i], moments[i], moments[6 + i], STEP_RATES[i], DECAY_RATES[i]
            )
            for i in range(6)
        ]
        return (
            block_output,
            input_grad,
            *owned,
            *(u[0] for u in updates),
            *(u[1] for u in updates),
            *(u[2] for u in updates),
        )

    return body


def solution(mesh):
    by_token = P("fsdp", "seq", None)
    by_row = P(BOTH, None)
    six = (by_row, by_row, by_row, by_row, P(None, BOTH), P(BOTH))
    return jax.shard_map(
        make_body(mesh.shape["seq"], mesh.shape["fsdp"]),
        mesh=mesh,
        in_specs=(by_token, by_token, P("fsdp")) + six * 3,
        out_specs=(by_token, by_token) + six * 4,
        check_vma=False,
    )
```

time: 1880 us -> 709 us (0.38)
  waiting for transfers between devices: 1190 us -> 182 us
  matrix products: 228 us -> 118 us
  local copies, waits for them, and re-layouts: 165 us -> 58.1 us
  Pallas kernels: 0 us -> 92 us
  starting transfers between devices: 17.7 us -> 60.6 us
  blocking collectives: 177 us -> 135 us
  other arithmetic: 77.4 us -> 37.7 us
    reduce_scatter x4 -> x0, waiting for transfers between devices: 1030 us -> none  [the longest x1 362 us: body(): lax.psum_scatter(grad_reduce, ('seq', 'fsdp'), scatter_dimension=0, tiled...]
    ppermute x0 -> x35, waiting for transfers between devices: none -> 112 us  [the longest x18 81.3 us: scatter_sum(): total = total + lax.ppermute(sent, axis, shift_pairs(count, step))]
    dot_general x33 -> x13, matrix products: 228 us -> 118 us  [the longest x5 51.2 us: dot(): return jnp.dot(left, right, preferred_element_type=F32)]
    pallas_call x0 -> x2, Pallas kernels: none -> 92 us  [the longest x1 58.3 us: attend_backward(): pl.pallas_call(kernel, out_shape=jax.ShapeDtypeStruct(joint.shape, BF16),...]
    all_to_all x4 -> x6, waiting for transfers between devices: 117 us -> 67.3 us  [the longest x1 27.1 us: body(): lax.all_to_all(attended_own, 'seq', split_axis=0, concat_axis=0, tiled=True)]
    reshape x8 -> x3, local copies, waits for them, and re-layouts: 50.2 us -> 3.18 us  [the longest x1 1.94 us: body(): own_joint.reshape(ns, own_rows, 3, own).transpose(1, 2, 0, 3)]
    unnamed x10 -> x7, waiting for transfers between devices: 44.4 us -> 2.63 us
    unnamed x1 -> x0, blocking collectives: 37.4 us -> none
  transfers between devices with their start and end apart: 13 -> 48, of which waited for: 8 -> 13; matrix products, arithmetic and copies ran while one was open for 13% -> 29% of each run, Pallas kernels for 0% -> 13%
where the time goes in v1:
time: 709 us; the launch traced here: 699 us
  waiting for transfers between devices  182 us (26%)
  blocking collectives  135 us (19%)
  matrix products  118 us (17%)
  Pallas kernels  92 us (13%)
  starting transfers between devices  60.6 us (9%)
  local copies, waits for them, and re-layouts  58.1 us (8%)
  other arithmetic  37.7 us (5%)
  between operations  15.4 us (2%)
    ppermute x18, waiting for transfers between devices, scatter_sum(): total = total + lax.ppermute(sent, axis, shift_pairs(count, step))  81.3 us
    all_gather x1, blocking collectives, body(): vector_rows = lax.all_gather(vectors, BOTH, axis=1, tiled=True).astype(F32)  71.1 us
    all_gather x1, blocking collectives, body(): lax.all_gather(expand_bias, BOTH, axis=0, tiled=True).astype(F32)  63.7 us
    pallas_call x1, Pallas kernels, attend_backward(): pl.pallas_call(kernel, out_shape=jax.ShapeDtypeStruct(joint.shape, BF16),...  58.3 us
    dot_general x5, matrix products, dot(): return jnp.dot(left, right, preferred_element_type=F32)  51.2 us
    dot_general x4, matrix products, dot_t(): lax.dot_general(left, right, (((1,), (1,)), ((), ())), preferred_element_...  41.5 us
    pallas_call x1, Pallas kernels, attend_forward(): pl.pallas_call(kernel, out_shape=jax.ShapeDtypeStruct(joint.shape[:3] + (...  33.6 us
    ppermute x3, waiting for transfers between devices, gather_ring(): got = lax.ppermute(piece, axis, shift_pairs(count, step))  30.8 us
  transfers between devices with their start and end apart: 48, of which 13 were waited for; matrix products, arithmetic and copies ran while one was open for 29% of the time, Pallas kernels for 13%

profile of v1, /device:TPU:0, one launch (start us, length us, event | category | flops | bytes accessed | tf_op | source)
XLA Modules:
  0.0 699.0 jit_solution(11793708004002205560)
XLA Ops:
  9.4 71.1 %all-gather = bf16[32,32,10]{1,2,0:T(8,128)(2,1)S(1)} all-gather(bf16[1,32,10]{1,2,0:T(8,128)(2,1)} %bitcast.348), channel_id=1, replica_groups=mesh['seq'=8,'fsdp'=4] {'seq','fsdp'}, dimensions={0}, use_global_device_ids=true | all-gather | bytes 21120 | tf_op jit(solution)/shard_map/all_gather | solution.py:316
  96.8 24.8 %all-to-all-done = bf16[8,32,3,128]{3,1,2,0:T(8,128)(2,1)S(1)} async-done(((bf16[8,32,3,128]{3,1,2,0:T(8,128)(2,1)}), bf16[8,32,3,128]{3,1,2,0:T(8,128)(2,1)S(1)}, u32[]{:S(2)}, u32[]{:S(2)}) %all-to-all-start) | async-done | bytes 196640 | tf_op jit(solution)/shard_map/all_to_all | solution.py:326
  122.8 8.4 %collective-permute-done.7 = bf16[8,32,3,128]{3,1,2,0:T(8,128)(2,1)S(1)} collective-permute-done((bf16[8,32,3,128]{3,1,2,0:T(8,128)(2,1)S(1)}, bf16[8,32,3,128]{3,1,2,0:T(8,128)(2,1)S(1)}, u32[]{:S(2)}, u32[]{:S(2)}) %collective-permute-start.7) | collective-permute-done | bytes 196640 | tf_op jit(solution)/shard_map/ppermute | solution.py:65
  132.6 14.8 %collective-permute-done.8 = bf16[8,32,3,128]{3,1,2,0:T(8,128)(2,1)S(1)} collective-permute-done((bf16[8,32,3,128]{3,1,2,0:T(8,128)(2,1)S(1)}, bf16[8,32,3,128]{3,1,2,0:T(8,128)(2,1)S(1)}, u32[]{:S(2)}, u32[]{:S(2)}) %collective-permute-start.8) | collective-permute-done | bytes 196640 | tf_op jit(solution)/shard_map/ppermute | solution.py:65
  149.1 7.6 %collective-permute-done.9 = bf16[8,32,3,128]{3,1,2,0:T(8,128)(2,1)S(1)} collective-permute-done((bf16[8,32,3,128]{3,1,2,0:T(8,128)(2,1)S(1)}, bf16[8,32,3,128]{3,1,2,0:T(8,128)(2,1)S(1)}, u32[]{:S(2)}, u32[]{:S(2)}) %collective-permute-start.9) | collective-permute-done | bytes 196640 | tf_op jit(solution)/shard_map/ppermute | solution.py:65
  167.6 9.5 %fusion.14 = bf16[4224,384]{1,0:T(8,128)(2,1)} fusion(bf16[4224,1024]{1,0:T(8,128)(2,1)} %bitcast.15, f32[384]{0:T(512)S(1)} %maximum_bitcast_fusion, bf16[128,8,3,128]{3,2,1,0:T(4,128)(2,1)S(1)} %bitcast.323), kind=kOutput, calls=%fused_computation.22 | convolution fusion | flops 3325132800 | bytes 12682752 | tf_op jit(solution)/shard_map/dot_general | solution.py:38
  178.2 33.6 %attend_forward.1 = bf16[8,3,176,128]{3,2,1,0:T(8,128)(2,1)} custom-call(s32[3]{0:T(128)} %refs_0_.3, s32[1408,128]{1,0:T(8,128)} %broadcast_in_dim.78.refs_1_, bf16[8,3,176,384]{3,2,1,0:T(8,128)(2,1)} %bitcast.305), custom_call_target="tpu_custom_call" | custom-call | tf_op jit(solution)/shard_map/attend_forward/pallas_call | solution.py:226
  215.9 27.1 %all-to-all-done.1 = bf16[8,528,128]{2,1,0:T(8,128)(2,1)S(1)} async-done(((bf16[8,528,128]{2,1,0:T(8,128)(2,1)}), bf16[8,528,128]{2,1,0:T(8,128)(2,1)S(1)}, u32[]{:S(2)}, u32[]{:S(2)}) %all-to-all-start.1) | async-done | bytes 1081376 | tf_op jit(solution)/shard_map/all_to_all | solution.py:354
  243.0 4.9 multiply_add_fusion
  255.7 63.7 %all-gather.1 = bf16[32,1,128]{2,1,0:T(2,128)(2,1)S(1)} all-gather(bf16[1,1,128]{2,1,0:T(2,128)(2,1)S(1)} %bitcast.364), channel_id=1, replica_groups=mesh['seq'=8,'fsdp'=4] {'seq','fsdp'}, dimensions={0}, use_global_device_ids=true | all-gather | bytes 8448 | tf_op jit(solution)/shard_map/all_gather | solution.py:317
  319.4 12.4 %fusion.112 = f32[528,4096]{1,0:T(8,128)} fusion(bf16[528,1024]{1,0:T(8,128)(2,1)} %add_convert_fusion.2, bf16[1024,4096]{1,0:T(8,128)(2,1)} %all-gather.12.cloned.1.call-done), kind=kOutput, calls=%fused_computation.231 | convolution fusion | flops 4429185024 | bytes 18120704 | tf_op jit(solution)/shard_map/dot_general | solution.py:38
  331.9 18.6 %multiply_reduce_fusion.1 = (f32[1024]{0:T(1024)S(1)}, f32[528]{0:T(1024)S(1)}, f32[1024]{0:T(1024)S(1)}, f32[528,1024]{1,0:T(8,128)}) fusion(f32[528,1024]{1,0:T(8,128)} %get-tuple-element.101, f32[528]{0:T(1024)S(1)} %fusion.89, f32[528]{0:T(1024)S(1)} %broadcast_multiply_fusion, f32[1024]{0:T(1024)S(1)} %bitcast.341, ...), kind=kOutput, calls=%fused_computation.42 | convolution fusion | flops 8886481920 | bytes 30869696 | tf_op jit(solution)/shard_map/dot_general | solution.py:46
  364.6 11.6 %copy.128 = bf16[1024,4224]{1,0:T(8,128)(2,1)} copy(bf16[1024,4224]{0,1:T(8,128)(2,1)} %bitcast.41) | data formatting | bytes 17301504 | tf_op jit(solution)/shard_map/dot_general | solution.py:42
  376.2 5.0 all-to-all-done.2
  381.3 58.3 %attend_backward.1 = bf16[8,3,176,384]{3,2,1,0:T(8,128)(2,1)} custom-call(s32[3]{0:T(128)} %refs_0_.3, s32[1408,128]{1,0:T(8,128)} %broadcast_in_dim.78.refs_1_, bf16[8,3,176,384]{3,2,1,0:T(8,128)(2,1)} %bitcast.306, bf16[8,3,176,128]{3,2,1,0:T(8,128)(2,1)} %bitcast.36.refs_3_), custom_call_target="tpu_custom_call" | custom-call | tf_op jit(solution)/shard_map/attend_backward/pallas_call | solution.py:252
  439.6 8.2 %fusion.113 = f32[8,4,32,384]{3,2,1,0:T(8,128)S(1)} fusion(bf16[8,4,32,4224]{3,2,1,0:T(8,128)(2,1)} %bitcast.309, bf16[4224,384,1,1]{1,0,3,2:T(8,128)(2,1)} %bitcast.302), kind=kOutput, calls=%fused_computation.232 | convolution fusion | flops 3321888768 | bytes 13467648 | tf_op jit(solution)/shard_map/dot_general | solution.py:42
  457.3 5.8 collective-permute-done.12
  463.1 22.7 %collective-permute-done.11 = f32[8,32,384]{2,1,0:T(8,128)} collective-permute-done((f32[8,32,384]{2,1,0:T(8,128)}, f32[8,32,384]{2,1,0:T(8,128)}, u32[]{:S(2)}, u32[]{:S(2)}) %collective-permute-start.11) | collective-permute-done | bytes 393248 | tf_op jit(solution)/shard_map/ppermute | solution.py:75
  494.9 10.3 %all-to-all-done.4 = f32[8,32,384]{2,1,0:T(8,128)} async-done(((f32[8,32,384]{2,1,0:T(8,128)}), f32[8,32,384]{2,1,0:T(8,128)}, u32[]{:S(2)}, u32[]{:S(2)}) %all-to-all-start.4) | async-done | bytes 393248 | tf_op jit(solution)/shard_map/all_to_all | solution.py:411
  505.1 4.8 all-to-all-start.3
  515.5 11.8 %fusion.31 = f32[4224,512]{1,0:T(8,128)} fusion(bf16[4224,1024]{1,0:T(8,128)(2,1)} %all-gather.20.cloned.1.call-done, bf16[1024,4096]{1,0:T(8,128)(2,1)} %all-gather.12.cloned.1.call-done, s32[]{:T(128)S(6)} %select_n.260), kind=kOutput, calls=%fused_computation.73 | convolution fusion | flops 4429185024 | bytes 18350084 | tf_op jit(solution)/shard_map/dot_general | solution.py:38
  527.3 12.4 %convert_reduce_fusion = (f32[512]{0:T(512)S(1)}, bf16[4224,512]{1,0:T(8,128)(2,1)S(1)}) fusion(f32[4224,512]{1,0:T(8,128)} %fusion.31, f32[512]{0:T(512)S(1)} %dynamic_slice.82, bf16[4224,1024]{1,0:T(8,128)(2,1)} %all-gather.22.cloned.1.call-done, bf16[4096,1024]{1,0:T(8,128)(2,1)} %all-gather.14.cloned.1.call-done, s32[]{:T(128)S(6)} %select_n.260), kind=kOutput, calls=%fused_computation.16 | convolution fusion | flops 4457299456 | bytes 22679556 | tf_op jit(solution)/shard_map/dot_general | solution.py:46
  539.7 4.8 fusion.114
  553.2 7.8 %fusion.16 = f32[512,1024]{1,0:T(8,128)S(1)} fusion(bf16[4224,1024]{1,0:T(8,128)(2,1)S(1)} %copy-done.31, f32[4224,512]{1,0:T(8,128)} %fusion.31, f32[512]{0:T(512)S(1)} %dynamic_slice.82), kind=kOutput, calls=%fused_computation.25 | convolution fusion | flops 4442161152 | bytes 19400704 | tf_op jit(solution)/shard_map/dot_general | solution.py:42
  563.4 5.6 copy.126
  569.1 6.3 copy.127
  575.3 7.2 %multiply_reduce_fusion.3 = (f32[1024]{0:T(1024)S(1)}, f32[528]{0:T(1024)S(1)}, f32[1024]{0:T(1024)S(1)}, f32[528,1024]{1,0:T(8,128)S(1)}) fusion(f32[528]{0:T(1024)S(1)} %rsqrt.20, f32[528]{0:T(1024)S(1)} %div.142, f32[3,176,1024]{2,1,0:T(8,128)S(1)} %pad_convert_fusion, f32[1024]{0:T(1024)S(1)} %bitcast.333, f32[528,1024]{1,0:T(8,128)S(1)} %bitcast.301, ...), kind=kOutput, calls=%fused_computation.45 | convolution fusion | flops 3326752256 | bytes 16042176 | tf_op jit(solution)/shard_map/dot_general | solution.py:46
  586.8 12.6 %multiply_reduce_fusion = (f32[1024]{0:T(1024)S(1)}, f32[1024]{0:T(1024)S(1)}, bf16[528,1024]{1,0:T(8,128)(2,1)}, bf16[528,1024]{1,0:T(8,128)(2,1)}) fusion(f32[528]{0:T(1024)S(1)} %reshape.472, f32[1024]{0:T(1024)S(1)} %bitcast.355, bf16[3,172,1024]{2,1,0:T(8,128)(2,1)S(1)} %copy-done.3, f32[528,1024]{1,0:T(8,128)} %get-tuple-element.102, ...), kind=kOutput, calls=%fused_computation.39 | convolution fusion | flops 4450809856 | bytes 28952768 | tf_op jit(solution)/shard_map/dot_general | solution.py:38
  624.6 10.1 %collective-permute-done.21 = f32[128,1024]{1,0:T(8,128)S(1)} collective-permute-done((f32[128,1024]{1,0:T(8,128)S(1)}, f32[128,1024]{1,0:T(8,128)S(1)}, u32[]{:S(2)}, u32[]{:S(2)}) %collective-permute-start.21) | collective-permute-done | bytes 524320 | tf_op jit(solution)/shard_map/ppermute | solution.py:75
  635.6 30.5 %collective-permute-done.20 = f32[128,1024]{1,0:T(8,128)} collective-permute-done((f32[128,1024]{1,0:T(8,128)S(1)}, f32[128,1024]{1,0:T(8,128)}, u32[]{:S(2)}, u32[]{:S(2)}) %collective-permute-start.20) | collective-permute-done | bytes 524320 | tf_op jit(solution)/shard_map/ppermute | solution.py:75
  670.5 4.9 fusion.12
  682.1 8.7 %collective-permute-done.14 = f32[32,1024]{1,0:T(8,128)S(1)} collective-permute-done((f32[32,1024]{1,0:T(8,128)S(1)}, f32[32,1024]{1,0:T(8,128)S(1)}, u32[]{:S(2)}, u32[]{:S(2)}) %collective-permute-start.14) | collective-permute-done | bytes 131104 | tf_op jit(solution)/shard_map/ppermute | solution.py:75
  (250 shorter events, 137.4 us)
Async XLA Ops:
  7.2 208.7 %all-gather.10.cloned.1.call-start = ((), (), s32[]{:S(2)}) async-start(), calls=%async_computation.6 | async-start | bytes 2162688 | tf_op jit(solution)/shard_map/all_gather | solution.py:342
  7.9 311.5 %all-gather.12.cloned.1.call-start = ((), (), s32[]{:S(2)}) async-start(), calls=%async_computation.7 | async-start | bytes 8650752 | tf_op jit(solution)/shard_map/all_gather | solution.py:343
  8.7 323.2 %all-gather.14.cloned.1.call-start = ((), (), s32[]{:S(2)}) async-start(), calls=%async_computation.8 | async-start | bytes 8650752 | tf_op jit(solution)/shard_map/all_gather | solution.py:344
  85.1 71.8 %collective-permute-start = (bf16[528,1024]{1,0:T(8,128)(2,1)}, bf16[528,1024]{1,0:T(8,128)(2,1)}, u32[]{:S(2)}, u32[]{:S(2)}) collective-permute-start(bf16[528,1024]{1,0:T(8,128)(2,1)} %add_convert_fusion.3), channel_id=1, source_target_pairs={{0,4},{4,0},{8,12},{12,8},{16,20},{20,16},{24,28},{28,24},{1,5},{5... | collective-permute-start | bytes 3244040 | tf_op jit(solution)/shard_map/ppermute | solution.py:96
  85.1 37.6 %collective-permute-start.1 = (bf16[528,1024]{1,0:T(8,128)(2,1)}, bf16[528,1024]{1,0:T(8,128)(2,1)}, u32[]{:S(2)}, u32[]{:S(2)}) collective-permute-start(bf16[528,1024]{1,0:T(8,128)(2,1)} %add_convert_fusion.3), channel_id=1, source_target_pairs={{0,8},{4,20},{8,0},{12,28},{16,24},{20,4},{24,16},{28,12},{1,9},{5... | collective-permute-start | bytes 3244040 | tf_op jit(solution)/shard_map/ppermute | solution.py:88
  85.1 71.7 %collective-permute-start.3 = (bf16[528,1024]{1,0:T(8,128)(2,1)}, bf16[528,1024]{1,0:T(8,128)(2,1)S(1)}, u32[]{:S(2)}, u32[]{:S(2)}) collective-permute-start(bf16[528,1024]{1,0:T(8,128)(2,1)} %add_convert_fusion.3), channel_id=1, source_target_pairs={{0,16},{4,12},{8,24},{12,4},{16,0},{20,28},{24,8},{28,20},{1,17},{... | collective-permute-start | bytes 3244040 | tf_op jit(solution)/shard_map/ppermute | solution.py:89
  86.4 35.2 %all-to-all-start = ((bf16[8,32,3,128]{3,1,2,0:T(8,128)(2,1)}), bf16[8,32,3,128]{3,1,2,0:T(8,128)(2,1)S(1)}, u32[]{:S(2)}, u32[]{:S(2)}) async-start(bf16[8,32,3,128]{3,1,2,0:T(8,128)(2,1)} %copy.119), calls=%async_computation | async-start | bytes 393216 | tf_op jit(solution)/shard_map/all_to_all | solution.py:326
  121.6 25.8 %collective-permute-start.8 = (bf16[8,32,3,128]{3,1,2,0:T(8,128)(2,1)S(1)}, bf16[8,32,3,128]{3,1,2,0:T(8,128)(2,1)S(1)}, u32[]{:S(2)}, u32[]{:S(2)}) collective-permute-start(bf16[8,32,3,128]{3,1,2,0:T(8,128)(2,1)S(1)} %all-to-all-done), channel_id=1, source_target_pairs={{0,2},{1,3},{2,0},{3,1},{4,6},{5,7},{6,4},{7,5},{8,10},{9,11},{10,... | collective-permute-start | bytes 589832 | tf_op jit(solution)/shard_map/ppermute | solution.py:65
  122.7 39.5 %collective-permute-start.2 = (bf16[528,1024]{1,0:T(8,128)(2,1)}, bf16[528,1024]{1,0:T(8,128)(2,1)S(1)}, u32[]{:S(2)}, u32[]{:S(2)}) collective-permute-start(bf16[528,1024]{1,0:T(8,128)(2,1)} %collective-permute-done.1), channel_id=1, source_target_pairs={{0,4},{4,0},{8,12},{12,8},{16,20},{20,16},{24,28},{28,24},{1,5},{5... | collective-permute-start | bytes 3244040 | tf_op jit(solution)/shard_map/ppermute | solution.py:96
  131.2 30.4 %collective-permute-start.5 = (bf16[528,1024]{1,0:T(8,128)(2,1)}, bf16[528,1024]{1,0:T(8,128)(2,1)S(1)}, u32[]{:S(2)}, u32[]{:S(2)}) collective-permute-start(bf16[528,1024]{1,0:T(8,128)(2,1)} %collective-permute-done.1), channel_id=1, source_target_pairs={{0,16},{4,12},{8,24},{12,4},{16,0},{20,28},{24,8},{28,20},{1,17},{... | collective-permute-start | bytes 3244040 | tf_op jit(solution)/shard_map/ppermute | solution.py:90
  211.9 31.1 %all-to-all-start.1 = ((bf16[8,528,128]{2,1,0:T(8,128)(2,1)}), bf16[8,528,128]{2,1,0:T(8,128)(2,1)S(1)}, u32[]{:S(2)}, u32[]{:S(2)}) async-start(bf16[8,528,128]{2,1,0:T(8,128)(2,1)} %bitcast.307), calls=%async_computation.1 | async-start | bytes 2162688 | tf_op jit(solution)/shard_map/all_to_all | solution.py:354
  215.6 299.9 %all-gather.20.cloned.1.call-start = ((), (), s32[]{:S(2)}) async-start(), calls=%async_computation.11 | async-start | bytes 9732096 | tf_op jit(solution)/shard_map/all_gather | solution.py:361
  253.6 273.8 %all-gather.22.cloned.1.call-start = ((), (), s32[]{:S(2)}) async-start(), calls=%async_computation.12 | async-start | bytes 9732096 | tf_op jit(solution)/shard_map/all_gather | solution.py:345
  255.1 320.2 %all-gather.16.cloned.1.call-start = ((), (), s32[]{:S(2)}) async-start(), calls=%async_computation.9 | async-start | bytes 6488064 | tf_op jit(solution)/shard_map/all_gather | solution.py:414
  359.8 21.4 %all-to-all-start.2 = ((bf16[8,528,128]{2,1,0:T(8,128)(2,1)}), bf16[8,528,128]{2,1,0:T(8,128)(2,1)}, u32[]{:S(2)}, u32[]{:S(2)}) async-start(bf16[8,528,128]{2,1,0:T(8,128)(2,1)} %bitcast.311), calls=%async_computation.2 | async-start | bytes 2162688 | tf_op jit(solution)/shard_map/all_to_all | solution.py:378
  364.1 306.3 %all-gather.18.cloned.1.call-start = ((), (), s32[]{:S(2)}) async-start(), calls=%async_computation.10 | async-start | bytes 9732096 | tf_op jit(solution)/shard_map/all_gather | solution.py:379
  453.3 32.6 %collective-permute-start.11 = (f32[8,32,384]{2,1,0:T(8,128)}, f32[8,32,384]{2,1,0:T(8,128)}, u32[]{:S(2)}, u32[]{:S(2)}) collective-permute-start(f32[8,32,384]{2,1,0:T(8,128)} %get-tuple-element.71), channel_id=1, source_target_pairs={{0,2},{1,3},{2,0},{3,1},{4,6},{5,7},{6,4},{7,5},{8,10},{9,11},{10,... | collective-permute-start | bytes 1179656 | tf_op jit(solution)/shard_map/ppermute | solution.py:75
  453.3 32.6 %collective-permute-start.10 = (f32[8,32,384]{2,1,0:T(8,128)}, f32[8,32,384]{2,1,0:T(8,128)}, u32[]{:S(2)}, u32[]{:S(2)}) collective-permute-start(f32[8,32,384]{2,1,0:T(8,128)} %get-tuple-element.69), channel_id=1, source_target_pairs={{0,1},{1,2},{2,3},{3,0},{4,5},{5,6},{6,7},{7,4},{8,9},{9,10},{10,1... | collective-permute-start | bytes 1179656 | tf_op jit(solution)/shard_map/ppermute | solution.py:75
  488.1 17.1 %all-to-all-start.4 = ((f32[8,32,384]{2,1,0:T(8,128)}), f32[8,32,384]{2,1,0:T(8,128)}, u32[]{:S(2)}, u32[]{:S(2)}) async-start(f32[8,32,384]{2,1,0:T(8,128)} %fusion.50), calls=%async_computation.4 | async-start | bytes 786432 | tf_op jit(solution)/shard_map/all_to_all | solution.py:411
  505.1 58.3 %all-to-all-start.3 = ((bf16[8,528,384]{2,1,0:T(8,128)(2,1)}), bf16[8,528,384]{2,1,0:T(8,128)(2,1)}, u32[]{:S(2)}, u32[]{:S(2)}) async-start(bf16[8,528,384]{2,1,0:T(8,128)(2,1)} %bitcast.303), calls=%async_computation.3 | async-start | bytes 6488064 | tf_op jit(solution)/shard_map/all_to_all | solution.py:415
  547.0 61.3 %collective-permute-start.18 = (f32[8,32,512]{2,1,0:T(8,128)}, f32[8,32,512]{2,1,0:T(8,128)}, u32[]{:S(2)}, u32[]{:S(2)}) collective-permute-start(f32[8,32,512]{2,1,0:T(8,128)} %get-tuple-element.68), channel_id=1, source_target_pairs={{0,3},{1,0},{2,1},{3,2},{4,7},{5,4},{6,5},{7,6},{8,11},{9,8},{10,9... | collective-permute-start | bytes 1572872 | tf_op jit(solution)/shard_map/ppermute | solution.py:75
  547.0 61.3 %collective-permute-start.17 = (f32[8,32,512]{2,1,0:T(8,128)}, f32[8,32,512]{2,1,0:T(8,128)}, u32[]{:S(2)}, u32[]{:S(2)}) collective-permute-start(f32[8,32,512]{2,1,0:T(8,128)} %get-tuple-element.67), channel_id=1, source_target_pairs={{0,2},{1,3},{2,0},{3,1},{4,6},{5,7},{6,4},{7,5},{8,10},{9,11},{10,... | collective-permute-start | bytes 1572872 | tf_op jit(solution)/shard_map/ppermute | solution.py:75
  549.3 59.6 %collective-permute-start.16 = (f32[8,32,512]{2,1,0:T(8,128)}, f32[8,32,512]{2,1,0:T(8,128)}, u32[]{:S(2)}, u32[]{:S(2)}) collective-permute-start(f32[8,32,512]{2,1,0:T(8,128)} %get-tuple-element.66), channel_id=1, source_target_pairs={{0,1},{1,2},{2,3},{3,0},{4,5},{5,6},{6,7},{7,4},{8,9},{9,10},{10,1... | collective-permute-start | bytes 1572872 | tf_op jit(solution)/shard_map/ppermute | solution.py:75
  551.3 48.2 %collective-permute-start.34 = (f32[128]{0:T(128)S(1)}, f32[128]{0:T(128)S(1)}, u32[]{:S(2)}, u32[]{:S(2)}) collective-permute-start(f32[128]{0:T(128)S(1)} %get-tuple-element.95), channel_id=1, source_target_pairs={{0,3},{1,0},{2,1},{3,2},{4,7},{5,4},{6,5},{7,6},{8,11},{9,8},{10,9... | collective-permute-start | bytes 1544 | tf_op jit(solution)/shard_map/ppermute | solution.py:75
  553.2 47.3 %collective-permute-start.33 = (f32[128]{0:T(128)S(1)}, f32[128]{0:T(128)S(1)}, u32[]{:S(2)}, u32[]{:S(2)}) collective-permute-start(f32[128]{0:T(128)S(1)} %get-tuple-element.96), channel_id=1, source_target_pairs={{0,2},{1,3},{2,0},{3,1},{4,6},{5,7},{6,4},{7,5},{8,10},{9,11},{10,... | collective-permute-start | bytes 1544 | tf_op jit(solution)/shard_map/ppermute | solution.py:75
  614.6 55.8 %all-to-all-start.5 = ((f32[8,32,512]{2,1,0:T(8,128)}), f32[8,32,512]{2,1,0:T(8,128)S(1)}, u32[]{:S(2)}, u32[]{:S(2)}) async-start(f32[8,32,512]{2,1,0:T(8,128)} %fusion.43), calls=%async_computation.5 | async-start | bytes 1048576 | tf_op jit(solution)/shard_map/all_to_all | solution.py:397
  618.5 16.2 %collective-permute-start.21 = (f32[128,1024]{1,0:T(8,128)S(1)}, f32[128,1024]{1,0:T(8,128)S(1)}, u32[]{:S(2)}, u32[]{:S(2)}) collective-permute-start(f32[128,1024]{1,0:T(8,128)S(1)} %copy-done.16), channel_id=1, source_target_pairs={{0,3},{1,0},{2,1},{3,2},{4,7},{5,4},{6,5},{7,6},{8,11},{9,8},{10,9... | collective-permute-start | bytes 1572872 | tf_op jit(solution)/shard_map/ppermute | solution.py:75
  619.3 46.8 %collective-permute-start.20 = (f32[128,1024]{1,0:T(8,128)S(1)}, f32[128,1024]{1,0:T(8,128)}, u32[]{:S(2)}, u32[]{:S(2)}) collective-permute-start(f32[128,1024]{1,0:T(8,128)S(1)} %copy-done.15), channel_id=1, source_target_pairs={{0,2},{1,3},{2,0},{3,1},{4,6},{5,7},{6,4},{7,5},{8,10},{9,11},{10,... | collective-permute-start | bytes 1572872 | tf_op jit(solution)/shard_map/ppermute | solution.py:75
  619.8 46.4 %collective-permute-start.19 = (f32[128,1024]{1,0:T(8,128)S(1)}, f32[128,1024]{1,0:T(8,128)}, u32[]{:S(2)}, u32[]{:S(2)}) collective-permute-start(f32[128,1024]{1,0:T(8,128)S(1)} %copy-done.14), channel_id=1, source_target_pairs={{0,1},{1,2},{2,3},{3,0},{4,5},{5,6},{6,7},{7,4},{8,9},{9,10},{10,1... | collective-permute-start | bytes 1572872 | tf_op jit(solution)/shard_map/ppermute | solution.py:75
  622.0 47.7 %collective-permute-start.31 = (f32[10,32]{1,0:T(8,128)S(1)}, f32[10,32]{1,0:T(8,128)S(1)}, u32[]{:S(2)}, u32[]{:S(2)}) collective-permute-start(f32[10,32]{1,0:T(8,128)S(1)} %bitcast.352), channel_id=1, source_target_pairs={{0,3},{1,0},{2,1},{3,2},{4,7},{5,4},{6,5},{7,6},{8,11},{9,8},{10,9... | collective-permute-start | bytes 3848 | tf_op jit(solution)/shard_map/ppermute | solution.py:75
  623.9 45.7 %collective-permute-start.30 = (f32[10,32]{1,0:T(8,128)S(1)}, f32[10,32]{1,0:T(8,128)S(1)}, u32[]{:S(2)}, u32[]{:S(2)}) collective-permute-start(f32[10,32]{1,0:T(8,128)S(1)} %bitcast.353), channel_id=1, source_target_pairs={{0,2},{1,3},{2,0},{3,1},{4,6},{5,7},{6,4},{7,5},{8,10},{9,11},{10,... | collective-permute-start | bytes 3848 | tf_op jit(solution)/shard_map/ppermute | solution.py:75
  635.5 34.2 %collective-permute-start.29 = (f32[10,32]{1,0:T(8,128)S(1)}, f32[10,32]{1,0:T(8,128)S(1)}, u32[]{:S(2)}, u32[]{:S(2)}) collective-permute-start(f32[10,32]{1,0:T(8,128)S(1)} %bitcast.354), channel_id=1, source_target_pairs={{0,1},{1,2},{2,3},{3,0},{4,5},{5,6},{6,7},{7,4},{8,9},{9,10},{10,1... | collective-permute-start | bytes 3848 | tf_op jit(solution)/shard_map/ppermute | solution.py:75
  (49 other events, 705.5 us)
Sparse Core Ops, SparseCore 0:
  10.9 59.1 all-gather.9
  73.0 93.9 all-gather.11
  169.9 85.9 all-gather.13
  258.2 55.1 all-gather.19
  315.2 56.8 all-gather.21
  374.8 78.9 all-gather.15
  455.6 58.8 all-gather.17

commit v2 on v1

--- a/solution.py
+++ b/solution.py
@@ -46,8 +46,8 @@
     return lax.dot_general(left, right, (((1,), (1,)), ((), ())), preferred_element_type=F32)
 
 
-def pick(stack, index):
-    return lax.dynamic_index_in_dim(stack, index, 0, keepdims=False)
+def pick(stack, index, axis=0):
+    return lax.dynamic_index_in_dim(stack, index, axis, keepdims=False)
 
 
 def place(stack, piece, index):
@@ -60,20 +60,28 @@
 
 def gather_ring(piece, axis, count):
     me = lax.axis_index(axis)
-    out = place(jnp.zeros((count,) + piece.shape, piece.dtype), piece, me)
+    out = jnp.broadcast_to(piece[None], (count,) + piece.shape)
     for step in range(1, count):
         got = lax.ppermute(piece, axis, shift_pairs(count, step))
         out = place(out, got, (me - step) % count)
     return out
 
 
-def scatter_sum(parts, axis, count):
+def scatter_sum(parts, axis, count, dim=0):
     me = lax.axis_index(axis)
-    total = pick(parts, me)
+    total = pick(parts, me, dim)
     for step in range(1, count):
-        sent = pick(parts, (me + step) % count)
+        sent = pick(parts, (me + step) % count, dim)
         total = total + lax.ppermute(sent, axis, shift_pairs(count, step))
     return total
+
+
+def swap(array):
+    return lax.all_to_all(array, "seq", split_axis=0, concat_axis=0, tiled=True)
+
+
+def side_by_side(blocks, start, size):
+    return [blocks[i, :, start : start + size] for i in range(blocks.shape[0])]
 
 
 def gather_plane(piece, count):
@@ -90,9 +98,10 @@
     three = lax.ppermute(one, "seq", pairs_two)
     mine = ((piece, me), (one, me ^ first), (two, me ^ second), (three, me ^ 6))
     theirs = (me ^ 1, me ^ 1 ^ second, me ^ 1 ^ first, me ^ 7)
-    out = jnp.zeros((8,) + piece.shape, piece.dtype)
+    out = jnp.broadcast_to(piece[None], (8,) + piece.shape)
     for (block, index), other in zip(mine, theirs):
-        out = place(out, block, index)
+        if block is not piece:
+            out = place(out, block, index)
         out = place(out, lax.ppermute(block, "seq", pairs_core), other)
     return out
 
@@ -313,35 +322,50 @@
         def unpadded(array):
             return array.reshape(images, pad_len, width)[:, :local_len]
 
-        vector_rows = lax.all_gather(vectors, BOTH, axis=1, tiled=True).astype(F32)
-        full_bias = lax.all_gather(expand_bias, BOTH, axis=0, tiled=True).astype(F32)
+        vector_size = vectors.size
+        small = jnp.concatenate([vectors.reshape(-1), expand_bias])
+        small = gather_ring(gather_ring(small, "fsdp", nf), "seq", ns)
+        vector_rows = small[:, :, :vector_size].reshape(ns, nf, vectors.shape[0], -1)
+        vector_rows = vector_rows.transpose(2, 0, 1, 3).reshape(vectors.shape[0], width).astype(F32)
+        full_bias = small[:, :, vector_size:].reshape(-1).astype(F32)
 
         features = padded(tokens).astype(F32)
         normed, norm_one_back = jax.vjp(norm_apply, features, vector_rows[0], vector_rows[1])
-        normed_low = normed.astype(BF16)
-        normed_all = gather_plane(normed_low, ns).reshape(ns * rows, width)
+        normed_low = normed.astype(BF16).reshape(images, pad_len, width)
+        normed_all = [
+            gather_plane(normed_low[i], ns).reshape(ns * pad_len, width) for i in range(images)
+        ]
 
         own_rows = joint_weight.shape[0]
-        pieces = joint_weight.reshape(own_rows, 3, ns, own).transpose(2, 0, 1, 3)
-        pieces = lax.all_to_all(pieces, "seq", split_axis=0, concat_axis=0, tiled=True)
-        pieces = gather_ring(pieces, "fsdp", nf)
-        joint_own = pieces.transpose(1, 0, 2, 3, 4).reshape(width, 3, own)
+        joint_z = gather_ring(joint_weight, "fsdp", nf).reshape(nf * own_rows, 3 * width)
+        output_z = gather_ring(output_weight, "fsdp", nf).reshape(-1, width)
+        expand_z = gather_ring(expand_weight, "fsdp", nf).reshape(-1, hidden)
+        reduce_z = gather_ring(reduce_weight, "fsdp", nf).reshape(-1, width)
+        pieces = jnp.stack(
+            [
+                jnp.concatenate(
+                    [joint_z[:, c * width + j * own : c * width + (j + 1) * own] for c in range(3)], axis=1
+                )
+                for j in range(ns)
+            ]
+        )
+        joint_own = swap(pieces).reshape(width, 3 * own)
         bias_own = lax.dynamic_slice_in_dim(vector_rows[2:4], seq * own, own, axis=1)
         bias_own = jnp.stack([bias_own[0], jnp.zeros_like(bias_own[0]), bias_own[1]])
         if lanes > own:
-            joint_own = jnp.pad(joint_own, ((0, 0), (0, 0), (0, lanes - own)))
+            joint_own = jnp.pad(joint_own.reshape(width, 3, own), ((0, 0), (0, 0), (0, lanes - own)))
+            joint_own = joint_own.reshape(width, 3 * lanes)
             bias_own = jnp.pad(bias_own, ((0, 0), (0, lanes - own)))
-        joint = dot(normed_all, joint_own.reshape(width, 3 * lanes)) + bias_own.reshape(-1)
-        joint = joint.astype(BF16).reshape(ns, images, pad_len, 3 * lanes)
+        bias_own = bias_own.reshape(-1)
 
         slot = jnp.arange(pad_len)
         live = (slot[None, :] < local_len) & (seq * local_len + slot[None, :] < lengths[:, None])
         grad_rows = padded(cotangent).astype(F32) * live.astype(F32).reshape(rows, 1)
         grad_reduced = (grad_rows * vector_rows[9]).astype(BF16)
 
-        full_output = lax.all_gather(output_weight, BOTH, axis=0, tiled=True)
-        full_expand = lax.all_gather(expand_weight, BOTH, axis=0, tiled=True)
-        full_reduce = lax.all_gather(reduce_weight, BOTH, axis=0, tiled=True)
+        full_expand = lax.all_gather(expand_z, "seq", axis=0, tiled=True)
+        full_reduce = lax.all_gather(reduce_z, "seq", axis=0, tiled=True)
+        full_output = gather_plane(output_z, ns).reshape(width, width)
         grad_reduced_all = lax.all_gather(grad_reduced, "seq", axis=0, tiled=True)
 
         index = jnp.arange(ns * pad_len)
@@ -349,10 +373,16 @@
             index % pad_len < local_len, (index // pad_len) * local_len + index % pad_len, 1 << 30
         ).astype(jnp.int32)
         positions = jnp.broadcast_to(position[:, None], (ns * pad_len, lanes))
-        attended = attend_forward(joint, lengths, positions, heads, lanes)
-        attended_own = attended.reshape(ns, rows, lanes)[:, :, :own]
-        attended_tok = lax.all_to_all(attended_own, "seq", split_axis=0, concat_axis=0, tiled=True)
-        attended_rows = attended_tok.transpose(1, 0, 2).reshape(rows, width)
+        joint = []
+        attended_own = []
+        attended_rows = []
+        for i in range(images):
+            made = (dot(normed_all[i], joint_own) + bias_own).astype(BF16)
+            joint.append(made.reshape(ns, 1, pad_len, 3 * lanes))
+            attended = attend_forward(joint[i], lengths[i : i + 1], positions, heads, lanes)
+            attended_own.append(attended.reshape(ns, pad_len, lanes)[:, :, :own])
+            attended_rows.append(jnp.concatenate(side_by_side(swap(attended_own[i]), 0, own), axis=1))
+        attended_rows = jnp.concatenate(attended_rows, axis=0)
 
         projected = dot(attended_rows, full_output) + vector_rows[4]
         hidden_one = features + vector_rows[5] * projected
@@ -374,54 +404,77 @@
         grad_projected = (grad_hidden * vector_rows[5]).astype(BF16)
         grad_output_bias = jnp.sum(grad_projected.astype(F32), axis=0)
         grad_attended = dot_t(grad_projected, full_output).astype(BF16)
-        grad_attended = grad_attended.reshape(rows, ns, own).transpose(1, 0, 2)
-        grad_heads = lax.all_to_all(grad_attended, "seq", split_axis=0, concat_axis=0, tiled=True)
-        grad_projected_all = lax.all_gather(grad_projected, "seq", axis=0, tiled=True)
-        if lanes > own:
-            grad_heads = jnp.pad(grad_heads, ((0, 0), (0, 0), (0, lanes - own)))
-        grad_heads = grad_heads.reshape(ns, images, pad_len, lanes)
+        grad_heads = []
+        for i in range(images):
+            part = grad_attended[i * pad_len : (i + 1) * pad_len]
+            part = swap(jnp.stack([part[:, j * own : (j + 1) * own] for j in range(ns)]))
+            if lanes > own:
+                part = jnp.pad(part, ((0, 0), (0, 0), (0, lanes - own)))
+            grad_heads.append(part.reshape(ns, 1, pad_len, lanes))
+        grad_projected_all = lax.all_gather(
+            grad_projected.reshape(images, pad_len, width), "seq", axis=0
+        )
 
         expand_own = lax.dynamic_slice_in_dim(full_expand, seq * slice_ff, slice_ff, axis=1)
-        reduce_own = lax.dynamic_slice_in_dim(full_reduce, seq * slice_ff, slice_ff, axis=0)
         ff_bias_own = lax.dynamic_slice_in_dim(full_bias, seq * slice_ff, slice_ff, axis=0)
         expanded_own = dot(normed_two_all, expand_own) + ff_bias_own
         activated_own, slope_own = gelu_parts(expanded_own)
-        grad_expanded_own = (dot_t(grad_reduced_all, reduce_own) * slope_own).astype(BF16)
+        grad_expanded_own = (dot_t(grad_reduced_all, reduce_z) * slope_own).astype(BF16)
         part_reduce = dot_rows(activated_own.astype(BF16), grad_reduced_all)
         part_expand = dot_rows(normed_two_all, grad_expanded_own)
         part_bias = jnp.sum(grad_expanded_own.astype(F32), axis=0)
+        grad_heads[0], part_reduce, part_expand = lax.optimization_barrier(
+            (grad_heads[0], part_reduce, part_expand)
+        )
         own_reduce = scatter_sum(part_reduce.reshape(nf, -1, width), "fsdp", nf)
-        own_expand = scatter_sum(
-            part_expand.reshape(ns, nf, own_rows, slice_ff).transpose(1, 0, 2, 3), "fsdp", nf
-        )
-        own_expand = lax.all_to_all(own_expand, "seq", split_axis=0, concat_axis=0, tiled=True)
-        own_expand = own_expand.transpose(1, 0, 2).reshape(own_rows, hidden)
+        own_expand = scatter_sum(part_expand.reshape(ns, nf, own_rows, slice_ff), "fsdp", nf, 1)
+        own_expand = jnp.concatenate(side_by_side(swap(own_expand), 0, slice_ff), axis=1)
         own_bias = scatter_sum(part_bias.reshape(nf, -1), "fsdp", nf)
 
-        grad_joint = attend_backward(joint, grad_heads, lengths, positions, heads, lanes)
-        part_output = dot_rows(attended_own.reshape(ns * rows, own), grad_projected_all)
+        part_joint = 0.0
+        part_output = 0.0
+        joint_sums = 0.0
+        grad_tok = []
+        for i in range(images):
+            made = attend_backward(joint[i], grad_heads[i], lengths[i : i + 1], positions, heads, lanes)
+            made = made.reshape(ns, pad_len, 3 * lanes)
+            if lanes > own:
+                made = jnp.concatenate(
+                    [made[:, :, c * lanes : c * lanes + own] for c in range(3)], axis=2
+                )
+            back = swap(made)
+            grad_tok.append(
+                jnp.concatenate(
+                    [block for c in range(3) for block in side_by_side(back, c * own, own)], axis=1
+                )
+            )
+            flat = made.reshape(ns * pad_len, 3 * own)
+            part_joint = part_joint + dot_rows(normed_all[i], flat)
+            joint_sums = joint_sums + jnp.sum(flat.astype(F32), axis=0)
+        own_joint = scatter_sum(part_joint.reshape(ns, nf, own_rows, 3 * own), "fsdp", nf, 1)
+        own_joint = swap(own_joint)
+        own_joint = jnp.concatenate(
+            [block for c in range(3) for block in side_by_side(own_joint, c * own, own)], axis=1
+        )
+        for i in range(images):
+            part_output = part_output + dot_rows(
+                attended_own[i].reshape(ns * pad_len, own),
+                grad_projected_all[:, i].reshape(ns * pad_len, width),
+            )
         own_output = scatter_sum(part_output.reshape(nf, -1, width), "fsdp", nf)
-        grad_joint_own = grad_joint.reshape(ns * rows, 3, lanes)[:, :, :own].reshape(ns, rows, 3 * own)
-        grad_joint_flat = grad_joint_own.reshape(ns * rows, 3 * own)
-        part_joint = dot_rows(normed_all, grad_joint_flat)
-        joint_sums = jnp.sum(grad_joint_flat.astype(F32), axis=0)
-        own_joint = scatter_sum(
-            part_joint.reshape(ns, nf, own_rows, 3 * own).transpose(1, 0, 2, 3), "fsdp", nf
-        )
-        own_joint = lax.all_to_all(own_joint, "seq", split_axis=0, concat_axis=0, tiled=True)
-        own_joint = own_joint.reshape(ns, own_rows, 3, own).transpose(1, 2, 0, 3).reshape(own_rows, 3 * width)
-
-        full_joint = lax.all_gather(joint_weight, BOTH, axis=0, tiled=True)
-        grad_tok = lax.all_to_all(grad_joint_own, "seq", split_axis=0, concat_axis=0, tiled=True)
-        grad_tok = grad_tok.reshape(ns, rows, 3, own).transpose(1, 2, 0, 3).reshape(rows, 3 * width)
-        grad_normed = dot_t(grad_tok, full_joint)
+
+        full_joint = lax.all_gather(joint_z, "seq", axis=0, tiled=True)
+        grad_normed = dot_t(jnp.concatenate(grad_tok, axis=0), full_joint)
         grad_input_part, grad_gain_one, grad_shift_one = norm_one_back(grad_normed)
         input_grad = unpadded((grad_hidden + grad_input_part).astype(BF16))
 
-        token_sums = jnp.stack(
+        def over_plane(sums):
+            sums = jnp.stack(sums).reshape(len(sums), ns, own)
+            return scatter_sum(sums, "seq", ns, 1)
+
+        late = over_plane([grad_gain_one, grad_shift_one])
+        early = over_plane(
             [
-                grad_gain_one,
-                grad_shift_one,
                 grad_output_bias,
                 grad_scale_one,
                 grad_gain_two,
@@ -430,13 +483,8 @@
                 grad_scale_two,
             ]
         )
-        token_sums = token_sums.reshape(8, ns, own).transpose(1, 0, 2)
-        plane_sums = pick(token_sums, seq)
-        for step in range(1, ns):
-            sent = pick(token_sums, (seq + step) % ns)
-            plane_sums = plane_sums + lax.ppermute(sent, "seq", shift_pairs(ns, step))
         plane_sums = jnp.concatenate(
-            [plane_sums[:2], joint_sums[None, :own], joint_sums[None, 2 * own :], plane_sums[2:]]
+            [late, joint_sums[None, :own], joint_sums[None, 2 * own :], early]
         )
         own_vectors = scatter_sum(plane_sums.reshape(10, nf, -1).transpose(1, 0, 2), "fsdp", nf)
 

time: 709 us -> 863 us (1.22)
  local copies, waits for them, and re-layouts: 58.1 us -> 212 us
  blocking collectives: 135 us -> 11 us
  starting transfers between devices: 60.6 us -> 178 us
  waiting for transfers between devices: 182 us -> 154 us
  matrix products: 118 us -> 133 us
  Pallas kernels: 92 us -> 104 us
    unnamed x73 -> x299, local copies, waits for them, and re-layouts: 5.19 us -> 149 us
    all_gather x2 -> x0, blocking collectives: 135 us -> none  [the longest x1 71.1 us: body(): vector_rows = lax.all_gather(vectors, BOTH, axis=1, tiled=True).astype(F32)]
    ppermute x18 -> x32, starting transfers between devices: 22.6 us -> 77.5 us  [scatter_sum(): total = total + lax.ppermute(sent, axis, shift_pairs(count, step))]
    all_to_all x6 -> x11, waiting for transfers between devices: 67.3 us -> 15.5 us  [swap(): return lax.all_to_all(array, 'seq', split_axis=0, concat_axis=0, tiled=True)]
    ppermute x3 -> x22, starting transfers between devices: 1.94 us -> 35.3 us  [gather_ring(): got = lax.ppermute(piece, axis, shift_pairs(count, step))]
    ppermute x1 -> x4, waiting for transfers between devices: 0.01 us -> 24.3 us  [gather_plane(): three = lax.ppermute(one, 'seq', pairs_two)]
    all_to_all x6 -> x11, starting transfers between devices: 24.9 us -> 46.3 us  [swap(): return lax.all_to_all(array, 'seq', split_axis=0, concat_axis=0, tiled=True)]
    ppermute x1 -> x4, waiting for transfers between devices: 0.01 us -> 16.7 us  [gather_plane(): one = lax.ppermute(piece, 'seq', pairs_one)]
  transfers between devices with their start and end apart: 48 -> 99, of which waited for: 13 -> 24; matrix products, arithmetic and copies ran while one was open for 29% -> 44% of each run, Pallas kernels for 13% -> 12%
where the time goes in v2:
time: 863 us; the launch traced here: 849 us
  local copies, waits for them, and re-layouts  212 us (25%)
  starting transfers between devices  178 us (21%)
  waiting for transfers between devices  154 us (18%)
  matrix products  133 us (15%)
  Pallas kernels  104 us (12%)
  other arithmetic  41.2 us (5%)
  between operations  16.5 us (2%)
  blocking collectives  11 us (1%)
    unnamed x299, local copies, waits for them, and re-layouts  149 us
    ppermute x32, starting transfers between devices, scatter_sum(): total = total + lax.ppermute(sent, axis, shift_pairs(count, step))  77.5 us
    ppermute x32, waiting for transfers between devices, scatter_sum(): total = total + lax.ppermute(sent, axis, shift_pairs(count, step))  69.6 us
    pallas_call x3, Pallas kernels, attend_backward(): pl.pallas_call(kernel, out_shape=jax.ShapeDtypeStruct(joint.shape, BF16),...  64.6 us
    dot_general x7, matrix products, dot(): return jnp.dot(left, right, preferred_element_type=F32)  56.4 us
    all_to_all x11, starting transfers between devices, swap(): return lax.all_to_all(array, 'seq', split_axis=0, concat_axis=0, tiled=True)  46.3 us
    dot_general x4, matrix products, dot_t(): lax.dot_general(left, right, (((1,), (1,)), ((), ())), preferred_element_...  43.3 us
    pallas_call x3, Pallas kernels, attend_forward(): pl.pallas_call(kernel, out_shape=jax.ShapeDtypeStruct(joint.shape[:3] + (...  39.3 us
  transfers between devices with their start and end apart: 99, of which 24 were waited for; matrix products, arithmetic and copies ran while one was open for 44% of the time, Pallas kernels for 12%

profile of v2, /device:TPU:0, one launch (start us, length us, event | category | flops | bytes accessed | tf_op | source)
XLA Modules:
  0.0 849.1 jit_solution(457626519599435373)
XLA Ops:
  14.3 5.6 collective-permute-done.44
  21.0 9.3 %collective-permute-done.45 = bf16[32,4096]{1,0:T(8,128)(2,1)S(1)} collective-permute-done((bf16[32,4096]{1,0:T(8,128)(2,1)}, bf16[32,4096]{1,0:T(8,128)(2,1)S(1)}, u32[]{:S(2)}, u32[]{:S(2)}) %collective-permute-start.45) | collective-permute-done | bytes 262176 | tf_op jit(solution)/shard_map/ppermute | solution.py:65
  31.6 6.0 collective-permute-start
  64.8 5.3 collective-permute-done.34
  122.6 13.1 %collective-permute-done.21 = bf16[176,1024]{1,0:T(8,128)(2,1)S(1)} collective-permute-done((bf16[176,1024]{1,0:T(8,128)(2,1)}, bf16[176,1024]{1,0:T(8,128)(2,1)S(1)}, u32[]{:S(2)}, u32[]{:S(2)}) %collective-permute-start.21) | collective-permute-done | bytes 360480 | tf_op jit(solution)/shard_map/ppermute | solution.py:96
  148.0 18.4 %collective-permute-done.42 = bf16[128,1024]{1,0:T(8,128)(2,1)S(1)} collective-permute-done((bf16[128,1024]{1,0:T(8,128)(2,1)}, bf16[128,1024]{1,0:T(8,128)(2,1)S(1)}, u32[]{:S(2)}, u32[]{:S(2)}) %collective-permute-start.42) | collective-permute-done | bytes 262176 | tf_op jit(solution)/shard_map/ppermute | solution.py:98
  195.3 13.1 %attend_forward.3 = bf16[8,1,176,128]{3,2,1,0:T(8,128)(2,1)} custom-call(s32[1]{0:T(128)} %get-tuple-element.163.refs_0_, s32[1408,128]{1,0:T(8,128)} %broadcast_in_dim.272.refs_1_, bf16[8,1,176,384]{3,2,1,0:T(8,128)(2,1)} %bitcast.1022), custom_call_target="tpu_custom_call" | custom-call | tf_op jit(solution)/shard_map/attend_forward/pallas_call | solution.py:235
  216.9 13.1 %attend_forward.4 = bf16[8,1,176,128]{3,2,1,0:T(8,128)(2,1)} custom-call(s32[1]{0:T(128)} %get-tuple-element.164.refs_0_, s32[1408,128]{1,0:T(8,128)} %broadcast_in_dim.272.refs_1_, bf16[8,1,176,384]{3,2,1,0:T(8,128)(2,1)} %bitcast.1026), custom_call_target="tpu_custom_call" | custom-call | tf_op jit(solution)/shard_map/attend_forward/pallas_call | solution.py:235
  235.4 13.1 %attend_forward.5 = bf16[8,1,176,128]{3,2,1,0:T(8,128)(2,1)} custom-call(s32[1]{0:T(128)} %get-tuple-element.165.refs_0_, s32[1408,128]{1,0:T(8,128)} %broadcast_in_dim.272.refs_1_, bf16[8,1,176,384]{3,2,1,0:T(8,128)(2,1)} %bitcast.1024), custom_call_target="tpu_custom_call" | custom-call | tf_op jit(solution)/shard_map/attend_forward/pallas_call | solution.py:235
  253.0 7.8 all-to-all-done.2
  264.5 7.7 all-to-all-done.3
  272.3 4.9 multiply_add_fusion
  285.2 12.7 %fusion.146 = f32[528,4096]{1,0:T(8,128)} fusion(bf16[528,1024]{1,0:T(8,128)(2,1)} %add_convert_fusion.2, bf16[1024,4096]{1,0:T(8,128)(2,1)} %all-gather.7.cloned.1.call-done), kind=kOutput, calls=%fused_computation.639 | convolution fusion | flops 4429185024 | bytes 18120704 | tf_op jit(solution)/shard_map/dot_general | solution.py:38
  297.9 18.6 %multiply_reduce_fusion.1 = (f32[1024]{0:T(1024)}, f32[528]{0:T(1024)}, f32[1024]{0:T(1024)}, f32[528,1024]{1,0:T(8,128)}) fusion(f32[528,1024]{1,0:T(8,128)S(1)} %get-tuple-element.166, f32[528]{0:T(1024)S(1)} %copy-done.55, f32[528]{0:T(1024)S(1)} %copy-done.36, f32[1024]{0:T(1024)S(1)} %copy-done.52, ...), kind=kOutput, calls=%fused_computation.47 | convolution fusion | flops 8886481920 | bytes 30869696 | tf_op jit(solution)/shard_map/dot_general | solution.py:46
  335.6 11.0 %all_to_all.60 = bf16[8,176,128]{2,1,0:T(8,128)(2,1)} all-to-all(bf16[8,176,128]{2,1,0:T(8,128)(2,1)S(1)} %get-tuple-element.79), channel_id=1, replica_groups=mesh['seq'=8,'fsdp'=4] {'seq'}, dimensions={0} | all-to-all | bytes 720896 | tf_op jit(solution)/shard_map/all_to_all | solution.py:80
  351.0 21.5 %attend_backward.4 = bf16[8,1,176,384]{3,2,1,0:T(8,128)(2,1)} custom-call(s32[1]{0:T(128)} %get-tuple-element.164.refs_0_, s32[1408,128]{1,0:T(8,128)} %broadcast_in_dim.272.refs_1_, bf16[8,1,176,384]{3,2,1,0:T(8,128)(2,1)} %bitcast.1027, bf16[8,1,176,128]{3,2,1,0:T(8,128)(2,1)} %bitcast.1044), custom_call_target="tpu_custom_call" | custom-call | tf_op jit(solution)/shard_map/attend_backward/pallas_call | solution.py:261
  378.8 21.5 %attend_backward.5 = bf16[8,1,176,384]{3,2,1,0:T(8,128)(2,1)} custom-call(s32[1]{0:T(128)} %get-tuple-element.165.refs_0_, s32[1408,128]{1,0:T(8,128)} %broadcast_in_dim.272.refs_1_, bf16[8,1,176,384]{3,2,1,0:T(8,128)(2,1)} %bitcast.1025, bf16[8,1,176,128]{3,2,1,0:T(8,128)(2,1)} %bitcast.178.refs_3_), custom_call_target="tpu_custom_call" | custom-call | tf_op jit(solution)/shard_map/attend_backward/pallas_call | solution.py:261
  403.4 4.7 fusion.149
  484.9 12.5 %fusion.39 = f32[4224,512]{1,0:T(8,128)} fusion(bf16[4224,1024]{1,0:T(8,128)(2,1)} %all-gather.11.cloned.1.call-done, bf16[1024,4096]{1,0:T(8,128)(2,1)} %all-gather.7.cloned.1.call-done, s32[]{:T(128)S(6)} %select_n.431), kind=kOutput, calls=%fused_computation.80 | convolution fusion | flops 4429185024 | bytes 18350084 | tf_op jit(solution)/shard_map/dot_general | solution.py:38
  497.5 12.2 %convert_reduce_fusion = (f32[512]{0:T(512)S(1)}, bf16[4224,512]{1,0:T(8,128)(2,1)S(1)}) fusion(f32[4224,512]{1,0:T(8,128)} %fusion.39, f32[512]{0:T(512)S(1)} %copy-done.76, bf16[4224,1024]{1,0:T(8,128)(2,1)} %all-gather.13.cloned.1.call-done, bf16[512,1024]{1,0:T(8,128)(2,1)} %bitcast.1030), kind=kOutput, calls=%fused_computation.14 | convolution fusion | flops 4457299456 | bytes 22679552 | tf_op jit(solution)/shard_map/dot_general | solution.py:46
  515.8 9.3 %fusion.13 = f32[512,1024]{1,0:T(8,128)} fusion(bf16[4224,1024]{1,0:T(8,128)(2,1)S(1)} %copy-done.78, f32[4224,512]{1,0:T(8,128)} %fusion.39, f32[512]{0:T(512)S(1)} %copy-done.76), kind=kOutput, calls=%fused_computation.20 | convolution fusion | flops 4442161152 | bytes 19400704 | tf_op jit(solution)/shard_map/dot_general | solution.py:42
  525.1 6.1 fusion.147
  531.2 21.5 %attend_backward.3 = bf16[8,1,176,384]{3,2,1,0:T(8,128)(2,1)} custom-call(s32[1]{0:T(128)} %get-tuple-element.163.refs_0_, s32[1408,128]{1,0:T(8,128)} %broadcast_in_dim.272.refs_1_, bf16[8,1,176,384]{3,2,1,0:T(8,128)(2,1)} %bitcast.1023, bf16[8,1,176,128]{3,2,1,0:T(8,128)(2,1)} %bitcast.109.refs_3_), custom_call_target="tpu_custom_call" | custom-call | tf_op jit(solution)/shard_map/attend_backward/pallas_call | solution.py:261
  570.1 12.3 %collective-permute-done.50 = f32[8,32,384]{2,1,0:T(8,128)S(1)} collective-permute-done((f32[8,32,384]{2,1,0:T(8,128)S(1)}, f32[8,32,384]{2,1,0:T(8,128)S(1)}, u32[]{:S(2)}, u32[]{:S(2)}) %collective-permute-start.50) | collective-permute-done | bytes 393248 | tf_op jit(solution)/shard_map/ppermute | solution.py:75
  585.7 13.7 %collective-permute-done.51 = f32[8,32,384]{2,1,0:T(8,128)} collective-permute-done((f32[8,32,384]{2,1,0:T(8,128)}, f32[8,32,384]{2,1,0:T(8,128)}, u32[]{:S(2)}, u32[]{:S(2)}) %collective-permute-start.51) | collective-permute-done | bytes 393248 | tf_op jit(solution)/shard_map/ppermute | solution.py:75
  599.4 27.3 %collective-permute-start.59 = (f32[128,1024]{1,0:T(8,128)}, f32[128,1024]{1,0:T(8,128)}, u32[]{:S(2)}, u32[]{:S(2)}) collective-permute-start(f32[128,1024]{1,0:T(8,128)} %get-tuple-element.68), channel_id=1, source_target_pairs={{0,1},{1,2},{2,3},{3,0},{4,5},{5,6},{6,7},{7,4},{8,9},{9,10},{10,1... | collective-permute-start | bytes 1572872 | tf_op jit(solution)/shard_map/ppermute | solution.py:75
  636.8 12.4 %collective-permute-done.57 = f32[8,32,512]{2,1,0:T(8,128)} collective-permute-done((f32[8,32,512]{2,1,0:T(8,128)}, f32[8,32,512]{2,1,0:T(8,128)}, u32[]{:S(2)}, u32[]{:S(2)}) %collective-permute-start.57) | collective-permute-done | bytes 524320 | tf_op jit(solution)/shard_map/ppermute | solution.py:75
  651.7 22.3 %collective-permute-done.60 = f32[128,1024]{1,0:T(8,128)} collective-permute-done((f32[128,1024]{1,0:T(8,128)}, f32[128,1024]{1,0:T(8,128)}, u32[]{:S(2)}, u32[]{:S(2)}) %collective-permute-start.60) | collective-permute-done | bytes 524320 | tf_op jit(solution)/shard_map/ppermute | solution.py:75
  751.3 9.2 %multiply_reduce_fusion.3 = (f32[1024]{0:T(1024)S(1)}, f32[528]{0:T(1024)S(1)}, f32[1024]{0:T(1024)S(1)}, f32[528,1024]{1,0:T(8,128)S(1)}) fusion(f32[528]{0:T(1024)S(1)} %copy-done.44, f32[528]{0:T(1024)S(1)} %copy-done.42, f32[3,176,1024]{2,1,0:T(8,128)} %copy-done, f32[1024]{0:T(1024)S(1)} %copy-done.38, f32[528,1024]{1,0:T(8,128)} %bitcast.1012, ...), kind=kOutput, calls=%fused_computation.53 | convolution fusion | flops 3336484352 | bytes 16042176 | tf_op jit(solution)/shard_map/dot_general | solution.py:46
  769.6 12.6 %multiply_reduce_fusion = (f32[1024]{0:T(1024)S(1)}, f32[1024]{0:T(1024)S(1)}, bf16[528,1024]{1,0:T(8,128)(2,1)}, bf16[528,1024]{1,0:T(8,128)(2,1)}) fusion(f32[528]{0:T(1024)S(1)} %copy-done.53, f32[1024]{0:T(1024)S(1)} %add.787, bf16[3,172,1024]{2,1,0:T(8,128)(2,1)S(1)} %copy-done.3, f32[528,1024]{1,0:T(8,128)} %get-tuple-element.167, ...), kind=kOutput, calls=%fused_computation.44 | convolution fusion | flops 4450809856 | bytes 28952768 | tf_op jit(solution)/shard_map/dot_general | solution.py:38
  794.9 11.7 %collective-permute-start.76 = (f32[10,32]{1,0:T(8,128)S(1)}, f32[10,32]{1,0:T(8,128)S(1)}, u32[]{:S(2)}, u32[]{:S(2)}) collective-permute-start(f32[10,32]{1,0:T(8,128)S(1)} %bitcast.1058), channel_id=1, source_target_pairs={{0,1},{1,2},{2,3},{3,0},{4,5},{5,6},{6,7},{7,4},{8,9},{9,10},{10,1... | collective-permute-start | bytes 3848 | tf_op jit(solution)/shard_map/ppermute | solution.py:75
  835.3 4.8 collective-permute-done.54
  (679 shorter events, 437.1 us)
Async XLA Ops:
  7.2 277.9 %all-gather.7.cloned.1.call-start = ((), (), s32[]{:S(2)}) async-start(), calls=%async_computation.12 | async-start | bytes 9437184 | tf_op jit(solution)/shard_map/all_gather | solution.py:366
  31.4 266.5 %all-gather.9.cloned.1.call-start = ((), (), s32[]{:S(2)}) async-start(), calls=%async_computation.13 | async-start | bytes 9437184 | tf_op jit(solution)/shard_map/all_gather | solution.py:367
  52.5 32.4 %collective-permute-start.18 = (bf16[32,3072]{1,0:T(8,128)(2,1)}, bf16[32,3072]{1,0:T(8,128)(2,1)}, u32[]{:S(2)}, u32[]{:S(2)}) collective-permute-start(bf16[32,3072]{1,0:T(8,128)(2,1)} %param.24), channel_id=1, source_target_pairs={{0,2},{1,3},{2,0},{3,1},{4,6},{5,7},{6,4},{7,5},{8,10},{9,11},{10,... | collective-permute-start | bytes 589832 | tf_op jit(solution)/shard_map/ppermute | solution.py:65
  54.9 31.0 %collective-permute-start.19 = (bf16[32,3072]{1,0:T(8,128)(2,1)}, bf16[32,3072]{1,0:T(8,128)(2,1)}, u32[]{:S(2)}, u32[]{:S(2)}) collective-permute-start(bf16[32,3072]{1,0:T(8,128)(2,1)} %param.24), channel_id=1, source_target_pairs={{0,3},{1,0},{2,1},{3,2},{4,7},{5,4},{6,5},{7,6},{8,11},{9,8},{10,9... | collective-permute-start | bytes 589832 | tf_op jit(solution)/shard_map/ppermute | solution.py:65
  85.9 31.6 %collective-permute-start.11 = (bf16[176,1024]{1,0:T(8,128)(2,1)}, bf16[176,1024]{1,0:T(8,128)(2,1)S(1)}, u32[]{:S(2)}, u32[]{:S(2)}) collective-permute-start(bf16[176,1024]{1,0:T(8,128)(2,1)} %get-tuple-element.101), channel_id=1, source_target_pairs={{0,8},{4,20},{8,0},{12,28},{16,24},{20,4},{24,16},{28,12},{1,9},{5... | collective-permute-start | bytes 1081352 | tf_op jit(solution)/shard_map/ppermute | solution.py:96
  93.0 76.4 %collective-permute-start.13 = (bf16[176,1024]{1,0:T(8,128)(2,1)}, bf16[176,1024]{1,0:T(8,128)(2,1)}, u32[]{:S(2)}, u32[]{:S(2)}) collective-permute-start(bf16[176,1024]{1,0:T(8,128)(2,1)} %get-tuple-element.101), channel_id=1, source_target_pairs={{0,16},{4,12},{8,24},{12,4},{16,0},{20,28},{24,8},{28,20},{1,17},{... | collective-permute-start | bytes 1081352 | tf_op jit(solution)/shard_map/ppermute | solution.py:97
  100.7 88.8 %all-to-all-start = ((bf16[8,128,384]{2,1,0:T(8,128)(2,1)}), bf16[8,128,384]{2,1,0:T(8,128)(2,1)}, u32[]{:S(2)}, u32[]{:S(2)}) async-start(bf16[8,128,384]{2,1,0:T(8,128)(2,1)} %constant_dynamic-update-slice_fusion), calls=%async_computation | async-start | bytes 1572864 | tf_op jit(solution)/shard_map/all_to_all | solution.py:80
  112.3 60.2 %collective-permute-start.23 = (bf16[176,1024]{1,0:T(8,128)(2,1)}, bf16[176,1024]{1,0:T(8,128)(2,1)S(1)}, u32[]{:S(2)}, u32[]{:S(2)}) collective-permute-start(bf16[176,1024]{1,0:T(8,128)(2,1)} %get-tuple-element.103), channel_id=1, source_target_pairs={{0,16},{4,12},{8,24},{12,4},{16,0},{20,28},{24,8},{28,20},{1,17},{... | collective-permute-start | bytes 1081352 | tf_op jit(solution)/shard_map/ppermute | solution.py:97
  142.3 33.0 %collective-permute-start.30 = (bf16[176,1024]{1,0:T(8,128)(2,1)S(1)}, bf16[176,1024]{1,0:T(8,128)(2,1)S(1)}, u32[]{:S(2)}, u32[]{:S(2)}) collective-permute-start(bf16[176,1024]{1,0:T(8,128)(2,1)S(1)} %get-tuple-element.102), channel_id=1, source_target_pairs={{0,16},{4,12},{8,24},{12,4},{16,0},{20,28},{24,8},{28,20},{1,17},{... | collective-permute-start | bytes 1081352 | tf_op jit(solution)/shard_map/ppermute | solution.py:97
  186.6 43.4 %collective-permute-start.33 = (bf16[176,1024]{1,0:T(8,128)(2,1)}, bf16[176,1024]{1,0:T(8,128)(2,1)}, u32[]{:S(2)}, u32[]{:S(2)}) collective-permute-start(bf16[176,1024]{1,0:T(8,128)(2,1)} %collective-permute-done.32), channel_id=1, source_target_pairs={{0,4},{4,0},{8,12},{12,8},{16,20},{20,16},{24,28},{28,24},{1,5},{5... | collective-permute-start | bytes 1081352 | tf_op jit(solution)/shard_map/ppermute | solution.py:105
  208.4 40.1 %all-to-all-start.1 = ((bf16[8,176,128]{2,1,0:T(8,128)(2,1)}), bf16[8,176,128]{2,1,0:T(8,128)(2,1)S(1)}, u32[]{:S(2)}, u32[]{:S(2)}) async-start(bf16[8,176,128]{2,1,0:T(8,128)(2,1)} %bitcast.1032), calls=%async_computation.1 | async-start | bytes 720896 | tf_op jit(solution)/shard_map/all_to_all | solution.py:80
  264.2 220.7 %all-gather.11.cloned.1.call-start = ((), (), s32[]{:S(2)}) async-start(), calls=%async_computation.14 | async-start | bytes 9732096 | tf_op jit(solution)/shard_map/all_gather | solution.py:391
  279.5 217.9 %all-gather.13.cloned.1.call-start = ((), (), s32[]{:S(2)}) async-start(), calls=%async_computation.15 | async-start | bytes 9732096 | tf_op jit(solution)/shard_map/all_gather | solution.py:369
  283.1 468.1 %all-gather.15.cloned.1.call-start = ((), (), s32[]{:S(2)}) async-start(), calls=%async_computation.16 | async-start | bytes 7077888 | tf_op jit(solution)/shard_map/all_gather | solution.py:466
  372.5 35.6 %all-to-all-start.7 = ((bf16[8,176,384]{2,1,0:T(8,128)(2,1)}), bf16[8,176,384]{2,1,0:T(8,128)(2,1)}, u32[]{:S(2)}, u32[]{:S(2)}) async-start(bf16[8,176,384]{2,1,0:T(8,128)(2,1)} %bitcast.1013), calls=%async_computation.7 | async-start | bytes 2162688 | tf_op jit(solution)/shard_map/all_to_all | solution.py:80
  376.8 442.3 %all-gather.17.cloned.1.call-start = ((), (), s32[]{:S(2)}) async-start(), calls=%async_computation.17 | async-start | bytes 9732096 | tf_op jit(solution)/shard_map/all_gather | solution.py:414
  408.1 38.3 %all-to-all-start.9 = ((bf16[8,176,384]{2,1,0:T(8,128)(2,1)}), bf16[8,176,384]{2,1,0:T(8,128)(2,1)}, u32[]{:S(2)}, u32[]{:S(2)}) async-start(bf16[8,176,384]{2,1,0:T(8,128)(2,1)} %bitcast.1017), calls=%async_computation.9 | async-start | bytes 2162688 | tf_op jit(solution)/shard_map/all_to_all | solution.py:80
  446.4 84.8 %all-to-all-start.4 = ((bf16[8,176,128]{2,1,0:T(8,128)(2,1)}), bf16[8,176,128]{2,1,0:T(8,128)(2,1)}, u32[]{:S(2)}, u32[]{:S(2)}) async-start(bf16[8,176,128]{2,1,0:T(8,128)(2,1)} %get-tuple-element.77), calls=%async_computation.4 | async-start | bytes 720896 | tf_op jit(solution)/shard_map/all_to_all | solution.py:80
  510.2 54.3 %collective-permute-start.79 = (f32[128]{0:T(128)}, f32[128]{0:T(128)}, u32[]{:S(2)}, u32[]{:S(2)}) collective-permute-start(f32[128]{0:T(128)} %get-tuple-element.156), channel_id=1, source_target_pairs={{0,1},{1,2},{2,3},{3,0},{4,5},{5,6},{6,7},{7,4},{8,9},{9,10},{10,1... | collective-permute-start | bytes 1544 | tf_op jit(solution)/shard_map/ppermute | solution.py:75
  511.9 56.1 %collective-permute-start.80 = (f32[128]{0:T(128)}, f32[128]{0:T(128)}, u32[]{:S(2)}, u32[]{:S(2)}) collective-permute-start(f32[128]{0:T(128)} %get-tuple-element.158), channel_id=1, source_target_pairs={{0,2},{1,3},{2,0},{3,1},{4,6},{5,7},{6,4},{7,5},{8,10},{9,11},{10,... | collective-permute-start | bytes 1544 | tf_op jit(solution)/shard_map/ppermute | solution.py:75
  514.2 54.0 %collective-permute-start.81 = (f32[128]{0:T(128)}, f32[128]{0:T(128)}, u32[]{:S(2)}, u32[]{:S(2)}) collective-permute-start(f32[128]{0:T(128)} %get-tuple-element.157), channel_id=1, source_target_pairs={{0,3},{1,0},{2,1},{3,2},{4,7},{5,4},{6,5},{7,6},{8,11},{9,8},{10,9... | collective-permute-start | bytes 1544 | tf_op jit(solution)/shard_map/ppermute | solution.py:75
  556.8 73.3 %collective-permute-start.56 = (f32[8,32,512]{2,1,0:T(8,128)}, f32[8,32,512]{2,1,0:T(8,128)}, u32[]{:S(2)}, u32[]{:S(2)}) collective-permute-start(f32[8,32,512]{2,1,0:T(8,128)} %get-tuple-element.71), channel_id=1, source_target_pairs={{0,1},{1,2},{2,3},{3,0},{4,5},{5,6},{6,7},{7,4},{8,9},{9,10},{10,1... | collective-permute-start | bytes 1572872 | tf_op jit(solution)/shard_map/ppermute | solution.py:75
  564.5 34.9 %collective-permute-start.51 = (f32[8,32,384]{2,1,0:T(8,128)}, f32[8,32,384]{2,1,0:T(8,128)}, u32[]{:S(2)}, u32[]{:S(2)}) collective-permute-start(f32[8,32,384]{2,1,0:T(8,128)} %get-tuple-element.76), channel_id=1, source_target_pairs={{0,2},{1,3},{2,0},{3,1},{4,6},{5,7},{6,4},{7,5},{8,10},{9,11},{10,... | collective-permute-start | bytes 1179656 | tf_op jit(solution)/shard_map/ppermute | solution.py:75
  568.0 58.7 %collective-permute-start.52 = (f32[8,32,384]{2,1,0:T(8,128)}, f32[8,32,384]{2,1,0:T(8,128)}, u32[]{:S(2)}, u32[]{:S(2)}) collective-permute-start(f32[8,32,384]{2,1,0:T(8,128)} %get-tuple-element.75), channel_id=1, source_target_pairs={{0,3},{1,0},{2,1},{3,2},{4,7},{5,4},{6,5},{7,6},{8,11},{9,8},{10,9... | collective-permute-start | bytes 1179656 | tf_op jit(solution)/shard_map/ppermute | solution.py:75
  568.2 81.0 %collective-permute-start.57 = (f32[8,32,512]{2,1,0:T(8,128)}, f32[8,32,512]{2,1,0:T(8,128)}, u32[]{:S(2)}, u32[]{:S(2)}) collective-permute-start(f32[8,32,512]{2,1,0:T(8,128)} %get-tuple-element.73), channel_id=1, source_target_pairs={{0,2},{1,3},{2,0},{3,1},{4,6},{5,7},{6,4},{7,5},{8,10},{9,11},{10,... | collective-permute-start | bytes 1572872 | tf_op jit(solution)/shard_map/ppermute | solution.py:75
  583.2 66.0 %collective-permute-start.58 = (f32[8,32,512]{2,1,0:T(8,128)}, f32[8,32,512]{2,1,0:T(8,128)}, u32[]{:S(2)}, u32[]{:S(2)}) collective-permute-start(f32[8,32,512]{2,1,0:T(8,128)} %get-tuple-element.72), channel_id=1, source_target_pairs={{0,3},{1,0},{2,1},{3,2},{4,7},{5,4},{6,5},{7,6},{8,11},{9,8},{10,9... | collective-permute-start | bytes 1572872 | tf_op jit(solution)/shard_map/ppermute | solution.py:75
  599.4 52.3 %collective-permute-start.59 = (f32[128,1024]{1,0:T(8,128)}, f32[128,1024]{1,0:T(8,128)}, u32[]{:S(2)}, u32[]{:S(2)}) collective-permute-start(f32[128,1024]{1,0:T(8,128)} %get-tuple-element.68), channel_id=1, source_target_pairs={{0,1},{1,2},{2,3},{3,0},{4,5},{5,6},{6,7},{7,4},{8,9},{9,10},{10,1... | collective-permute-start | bytes 1572872 | tf_op jit(solution)/shard_map/ppermute | solution.py:75
  626.7 47.3 %collective-permute-start.60 = (f32[128,1024]{1,0:T(8,128)}, f32[128,1024]{1,0:T(8,128)}, u32[]{:S(2)}, u32[]{:S(2)}) collective-permute-start(f32[128,1024]{1,0:T(8,128)} %get-tuple-element.70), channel_id=1, source_target_pairs={{0,2},{1,3},{2,0},{3,1},{4,6},{5,7},{6,4},{7,5},{8,10},{9,11},{10,... | collective-permute-start | bytes 1572872 | tf_op jit(solution)/shard_map/ppermute | solution.py:75
  630.1 43.9 %collective-permute-start.61 = (f32[128,1024]{1,0:T(8,128)}, f32[128,1024]{1,0:T(8,128)}, u32[]{:S(2)}, u32[]{:S(2)}) collective-permute-start(f32[128,1024]{1,0:T(8,128)} %get-tuple-element.69), channel_id=1, source_target_pairs={{0,3},{1,0},{2,1},{3,2},{4,7},{5,4},{6,5},{7,6},{8,11},{9,8},{10,9... | collective-permute-start | bytes 1572872 | tf_op jit(solution)/shard_map/ppermute | solution.py:75
  632.3 44.9 %all-to-all-start.10 = ((f32[8,32,384]{2,1,0:T(8,128)}), f32[8,32,384]{2,1,0:T(8,128)}, u32[]{:S(2)}, u32[]{:S(2)}) async-start(f32[8,32,384]{2,1,0:T(8,128)} %fusion.55), calls=%async_computation.10 | async-start | bytes 786432 | tf_op jit(solution)/shard_map/all_to_all | solution.py:80
  677.2 36.1 %all-to-all-start.5 = ((bf16[8,176,384]{2,1,0:T(8,128)(2,1)}), bf16[8,176,384]{2,1,0:T(8,128)(2,1)}, u32[]{:S(2)}, u32[]{:S(2)}) async-start(bf16[8,176,384]{2,1,0:T(8,128)(2,1)} %bitcast.1015), calls=%async_computation.5 | async-start | bytes 2162688 | tf_op jit(solution)/shard_map/all_to_all | solution.py:80
  713.3 99.0 %all-to-all-start.11 = ((f32[8,32,512]{2,1,0:T(8,128)}), f32[8,32,512]{2,1,0:T(8,128)}, u32[]{:S(2)}, u32[]{:S(2)}) async-start(f32[8,32,512]{2,1,0:T(8,128)} %fusion.50), calls=%async_computation.11 | async-start | bytes 1048576 | tf_op jit(solution)/shard_map/all_to_all | solution.py:80
  (150 other events, 1903.4 us)
Sparse Core Ops, SparseCore 0:
  31.5 59.3 all-gather.6
  100.2 79.1 all-gather.8
  279.6 54.4 all-gather.10
  335.9 70.8 all-gather.12
  408.5 57.1 all-gather.14
  467.5 55.3 all-gather.16
